TPU v7x, 256 devices: a whole 4x4x8 slice. The times are simulated.
256 devices in a mesh: group: 2 (over z_hi), ctx: 16 (over z_lo, y), tp: 8 (over x, core).
Axes of the slice: x: 4, y: 4, z: 8 (z_hi: 2, z_lo: 4; z = z_hi * 4 + z_lo), core: 2. Of those that a mesh axis runs over, the one named last changes fastest.
Arguments:
- stretch_query: bfloat16 [2, 2048, 8192], P('group', 'ctx', 'tp'), may hold values from -8 to 8
- prefix_keyvals: bfloat16 [2, 2, 16384, 1024], P('group', None, 'ctx', 'tp'), may hold values from -6 to 6
- stretch_key_values: bfloat16 [2, 2, 2048, 1024], P('group', None, 'ctx', 'tp'), may hold values from -6 to 6
- stretch_start: int32 [2], P('group'), may hold values from 4096 to 16384
- decode_query: bfloat16 [512, 4, 8192], P(('group', 'ctx'), None, 'tp'), may hold values from -8 to 8
- draft_key_values: bfloat16 [2, 512, 4, 1024], P(None, ('group', 'ctx'), None, 'tp'), may hold values from -6 to 6
- decode_cache: bfloat16 [2, 512, 1024, 1024], P(None, ('group', 'ctx'), None, 'tp'), may hold values from -6 to 6
- cache_lengths: int32 [512], P(('group', 'ctx')), may hold values from 128 to 1024, as said below
- page_rows: int32 [32], replicated, may hold values from 0 to 511, as said below
Outputs:
- prefill_out: bfloat16 [2, 2048, 8192], P('group', 'ctx', 'tp')
- decode_out: bfloat16 [512, 4, 8192], P(('group', 'ctx'), None, 'tp')
Inputs may be any that keep to these rules, and one draw needn't show every extreme that they name: `cache_lengths`: one row has length 1024. `page_rows`: page n = g * 16 + c names one of the rows m * 16 to m * 16 + 15, where m = (n + 1) mod 32 if n mod 4 = 1, m = g * 16 + (c + 16 / 2) mod 16 if n mod 4 = 3, and m = (n + 16) mod 32 for even n; no row is named twice.
All inputs are finite; a program needn't handle non-finite values.
Results may differ from a plain program's by a relative error of at most 0.0049.
Values may be sent and summed in bfloat16 or wider, within the bound.
No kernel may reach another device: no remote copies, remote signals or barrier semaphores. Data moves between devices by JAX's collectives and lax.ppermute only.
A program may use at most 128 MiB of HBM per device.

v0:
```python
import math

import jax
import jax.numpy as jnp
from jax import lax
from jax.sharding import PartitionSpec as P

QUERY_HEADS = 64
KEY_VALUE_HEADS = 8
HEAD_SIZE = 128


def joined_along(tiles, dim):
    lengths = list(tiles.shape[1:])
    lengths[dim] *= tiles.shape[0]
    return jnp.moveaxis(tiles, 0, dim).reshape(lengths)


def copy_for_each(x, axis):
    copies = jnp.broadcast_to(x, (lax.axis_size(axis), *x.shape))
    return lax.all_to_all(copies, axis, split_axis=0, concat_axis=0, tiled=True)


def gather_directly(x, axis, dim):
    return joined_along(copy_for_each(x, axis), dim)


def refresh(maxima, totals, scores, allowed):
    masked = jnp.where(allowed, scores, -jnp.inf)
    highest = jnp.maximum(maxima, jnp.max(masked, axis=-1))
    anchor = jnp.where(highest == -jnp.inf, 0.0, highest)
    weights = jnp.exp(masked - anchor[..., None])
    factor = jnp.exp(maxima - anchor)
    totals = totals * factor + jnp.sum(weights, axis=-1)
    return (highest, totals, weights.astype(jnp.bfloat16), factor)


def prefill_folder(queries, query_pos, limit, causal, inv_root, running, shard_piece):
    heads_local = queries.shape[1]
    piece_rows = shard_piece.shape[2]
    block_size = 512

    def absorb_step(block_index, carry):
        maxima, totals, summed = carry
        offset = block_index * block_size
        block = lax.dynamic_slice_in_dim(shard_piece, offset, block_size, 2)
        key_block = block[0, 0].reshape(block_size, heads_local, HEAD_SIZE)
        value_block = block[0, 1].reshape(block_size, heads_local, HEAD_SIZE)
        scores = (
            jnp.einsum("tkgd,skd->kgts", queries, key_block, preferred_element_type=jnp.float32)
            * inv_root
        )
        key_pos = offset + jnp.arange(block_size, dtype=jnp.int32)
        if causal:
            allowed = key_pos[None, :] <= query_pos[:, None]
        else:
            allowed = (key_pos < limit)[None, :]
        maxima, totals, weights, factor = refresh(maxima, totals, scores, allowed)
        summed = summed * factor[..., None] + jnp.einsum(
            "kgts,skd->kgtd", weights, value_block, preferred_element_type=jnp.float32
        )
        return (maxima, totals, summed)

    return lax.fori_loop(0, piece_rows // block_size, absorb_step, running)


def on_device(
    stretch_query,
    prefix_keyvals,
    stretch_key_values,
    stretch_start,
    decode_query,
    draft_key_values,
    decode_cache,
    cache_lengths,
    page_rows,
):
    grouped_query = QUERY_HEADS // KEY_VALUE_HEADS
    inv_root = 1.0 / math.sqrt(HEAD_SIZE)
    stretch_rows = stretch_query.shape[1]
    heads_local = stretch_key_values.shape[3] // HEAD_SIZE
    queries = stretch_query[0].reshape(stretch_rows, heads_local, grouped_query, HEAD_SIZE)
    ctx_index = lax.axis_index("ctx")
    query_pos = ctx_index * stretch_rows + jnp.arange(stretch_rows, dtype=jnp.int32)
    limit = stretch_start[0]
    state_shape = (heads_local, grouped_query, stretch_rows)
    running = (
        jnp.full(state_shape, -jnp.inf, jnp.float32),
        jnp.zeros(state_shape, jnp.float32),
        jnp.zeros(state_shape + (HEAD_SIZE,), jnp.float32),
    )
    running = prefill_folder(
        queries,
        query_pos,
        limit,
        False,
        inv_root,
        running,
        lax.all_gather(prefix_keyvals, "ctx", axis=2, tiled=True),
    )
    maxima, totals, summed = prefill_folder(
        queries,
        query_pos,
        limit,
        True,
        inv_root,
        running,
        gather_directly(stretch_key_values, "ctx", 2),
    )
    attended = summed / totals[..., None]
    prefill_out = (
        attended.transpose(2, 0, 1, 3)
        .reshape(1, stretch_rows, heads_local * grouped_query * HEAD_SIZE)
        .astype(jnp.bfloat16)
    )
    within = gather_directly(stretch_key_values, "ctx", 0)
    pages = gather_directly(within, "group", 0)
    row_count = decode_query.shape[0]
    steps = decode_query.shape[1]
    page_size = stretch_key_values.shape[2]
    decode_heads = decode_query.reshape(row_count, steps, heads_local, grouped_query, HEAD_SIZE)
    row_ids = lax.axis_index(("group", "ctx")) * row_count + jnp.arange(row_count, dtype=jnp.int32)
    matches = row_ids[:, None] == page_rows[None, :]
    has_page = jnp.any(matches, axis=1)
    page_block = jnp.einsum(
        "rp,pcsd->crsd", matches.astype(jnp.bfloat16), pages, preferred_element_type=jnp.float32
    ).astype(jnp.bfloat16)
    first_block = jnp.where(
        has_page[None, :, None, None], page_block, decode_cache[:, :, :page_size]
    )

    def absorb(carry, block, allowed):
        maxima, totals, summed = carry
        block_rows = block.shape[2]
        key_block = block[0].reshape(row_count, block_rows, heads_local, HEAD_SIZE)
        value_block = block[1].reshape(row_count, block_rows, heads_local, HEAD_SIZE)
        scores = (
            jnp.einsum(
                "rtkgd,rskd->rkgts", decode_heads, key_block, preferred_element_type=jnp.float32
            )
            * inv_root
        )
        maxima, totals, weights, factor = refresh(maxima, totals, scores, allowed)
        summed = summed * factor[..., None] + jnp.einsum(
            "rkgts,rskd->rkgtd", weights, value_block, preferred_element_type=jnp.float32
        )
        return (maxima, totals, summed)

    def cache_allowed(offset):
        positions = offset + jnp.arange(page_size, dtype=jnp.int32)
        return (positions[None, :] < cache_lengths[:, None])[:, None, None, None, :]

    decode_shape = (row_count, heads_local, grouped_query, steps)
    running = (
        jnp.full(decode_shape, -jnp.inf, jnp.float32),
        jnp.zeros(decode_shape, jnp.float32),
        jnp.zeros(decode_shape + (HEAD_SIZE,), jnp.float32),
    )
    running = absorb(running, first_block, cache_allowed(0))

    def cache_step(block_index, carry):
        offset = block_index * page_size
        block = lax.dynamic_slice_in_dim(decode_cache, offset, page_size, 2)
        return absorb(carry, block, cache_allowed(offset))

    upper = decode_cache.shape[2] // page_size
    running = lax.fori_loop(1, upper, cache_step, running)
    step_pos = jnp.arange(steps, dtype=jnp.int32)
    draft_allowed = (step_pos[None, :] <= step_pos[:, None])[None, None, None, :, :]
    maxima, totals, summed = absorb(running, draft_key_values, draft_allowed)
    decoded = summed / totals[..., None]
    decode_out = (
        decoded.transpose(0, 3, 1, 2, 4)
        .reshape(row_count, steps, heads_local * grouped_query * HEAD_SIZE)
        .astype(jnp.bfloat16)
    )
    return (prefill_out, decode_out)


def solution(mesh):
    return jax.shard_map(
        on_device,
        mesh=mesh,
        in_specs=(
            P("group", "ctx", "tp"),
            P("group", None, "ctx", "tp"),
            P("group", None, "ctx", "tp"),
            P("group"),
            P(("group", "ctx"), None, "tp"),
            P(None, ("group", "ctx"), None, "tp"),
            P(None, ("group", "ctx"), None, "tp"),
            P(("group", "ctx")),
            P(),
        ),
        out_specs=(P("group", "ctx", "tp"), P(("group", "ctx"), None, "tp")),
        check_vma=False,
    )
```

profile of v0, /device:TPU:2, one launch (start us, length us, event | category | flops | bytes accessed | tf_op | source)
XLA Modules:
  0.0 352.9 jit_solution(2781687481947533330)
XLA Ops:
  8.2 35.1 %all_to_all.11 = bf16[16,1,2,128,128]{4,3,2,1,0:T(8,128)(2,1)S(1)} all-to-all(bf16[16,1,2,128,128]{4,3,2,1,0:T(8,128)(2,1)S(1)} %broadcast_in_dim.189), channel_id=1, replica_groups=mesh['group'=2,'ctx'=16,'tp'=8] {'ctx'}, dimensions={0} | all-to-all | bytes 2097152 | tf_op jit(solution)/shard_map/all_to_all | solution.py:21
  45.6 5.9 %all-to-all-start.1 = ((bf16[2,16,2,128,128]{4,1,3,2,0:T(8,128)(2,1)}), bf16[2,16,2,128,128]{4,1,3,2,0:T(8,128)(2,1)}, u32[]{:S(2)}, u32[]{:S(2)}) async-start(bf16[2,16,2,128,128]{4,1,3,2,0:T(8,128)(2,1)} %broadcast_in_dim.192), calls=%async_computation.1 | async-start | bytes 4194304 | tf_op jit(solution)/shard_map/all_to_all | solution.py:21
  54.9 35.2 %all-to-all-done.1 = bf16[2,16,2,128,128]{4,1,3,2,0:T(8,128)(2,1)} async-done(((bf16[2,16,2,128,128]{4,1,3,2,0:T(8,128)(2,1)}), bf16[2,16,2,128,128]{4,1,3,2,0:T(8,128)(2,1)}, u32[]{:S(2)}, u32[]{:S(2)}) %all-to-all-start.1) | async-done | bytes 2097184 | tf_op jit(solution)/shard_map/all_to_all | solution.py:21
  90.2 2.0 copy.47
  94.4 23.9 %while.53 = (s32[]{:T(128)}, f32[16,1,8,4]{2,3,0,1:T(4,128)S(1)}, f32[16,1,8,4]{2,3,0,1:T(4,128)S(1)}, f32[16,1,8,4,128]{4,2,3,0,1:T(8,128)S(1)}, s32[16]{0:T(12...) while((s32[]{:T(128)}, f32[16,1,8,4]{2,3,0,1:T(4,128)S(1)}, ...), condition=%wide.region_14.15_spmd, body=%wide.region_11.14_spmd.sunk | while | flops 34151044 | bytes 2532607 | solution.py:167
  119.5 67.1 %all-gather.2.cloned.1.call-done = bf16[1,2,16384,128]{3,2,1,0:T(8,128)(2,1)} async-done(((bf16[1,2,1024,128]{3,2,1,0:T(8,128)(2,1)}), bf16[1,2,16384,128]{3,2,1,0:T(8,128)(2,1)}) %all-gather.2.cloned.1.call-update) | async-done | bytes 8388624 | tf_op jit(solution)/shard_map/all_gather | solution.py:99
  186.6 144.1 %while.55 = (s32[]{:T(128)}, f32[1,8,128]{2,1,0:T(8,128)S(1)}, f32[1,8,128]{2,1,0:T(8,128)S(1)}, f32[1,8,128,128]{3,2,1,0:T(8,128)S(1)}, s32[]{:T(128)}, /*index...) while((s32[]{:T(128)}, f32[1,8,128]{2,1,0:T(8,128)S(1)}, ...), condition=%wide.region_3.4_spmd.clone, body=%wide.region_0.3_spmd.clone.sunk | while | flops 274609152 | bytes 7940311 | solution.py:64
  193.7 1.9 fusion.123
  198.2 1.9 fusion.123
  202.7 1.9 fusion.123
  207.2 1.9 fusion.123
  211.7 1.9 fusion.123
  220.7 1.9 fusion.123
  225.2 1.9 fusion.123
  229.8 1.9 fusion.123
  234.3 1.9 fusion.123
  238.8 1.9 fusion.123
  247.8 1.9 fusion.123
  252.3 1.9 fusion.123
  256.8 1.9 fusion.123
  261.3 1.9 fusion.123
  265.8 1.9 fusion.123
  274.8 1.9 fusion.123
  279.3 1.9 fusion.123
  288.3 1.9 fusion.123
  292.8 1.9 fusion.123
  301.8 1.9 fusion.123
  306.3 1.9 fusion.123
  315.4 1.9 fusion.123
  319.9 1.9 fusion.123
  328.9 1.9 fusion.123
  330.8 14.1 %while.54 = (s32[]{:T(128)}, f32[1,8,128]{2,1,0:T(8,128)S(1)}, f32[1,8,128]{2,1,0:T(8,128)S(1)}, f32[1,8,128,128]{3,2,1,0:T(8,128)S(1)}, bf16[1,2,2048,128]{3,2,...) while((s32[]{:T(128)}, f32[1,8,128]{2,1,0:T(8,128)S(1)}, ...), condition=%wide.region_7.8_spmd.clone, body=%wide.region_4.7_spmd.clone.sunk | while | flops 272443008 | bytes 8074443 | solution.py:64
  (380 shorter events, 144.6 us)
Async XLA Ops:
  45.6 6.7 %copy-start = (bf16[16,4,1024]{2,1,0:T(4,128)(2,1)S(1)}, bf16[16,4,1024]{2,1,0:T(4,128)(2,1)}, u32[]{:S(2)}) copy-start(bf16[16,4,1024]{2,1,0:T(4,128)(2,1)} %param.19) | copy-start | bytes 393220
  45.6 6.8 %copy-start.1 = (bf16[1,128,1024]{2,1,0:T(8,128)(2,1)S(1)}, bf16[1,128,1024]{2,1,0:T(8,128)(2,1)}, u32[]{:S(2)}) copy-start(bf16[1,128,1024]{2,1,0:T(8,128)(2,1)} %param.15) | copy-start | bytes 786436
  45.6 44.6 %all-to-all-start.1 = ((bf16[2,16,2,128,128]{4,1,3,2,0:T(8,128)(2,1)}), bf16[2,16,2,128,128]{4,1,3,2,0:T(8,128)(2,1)}, u32[]{:S(2)}, u32[]{:S(2)}) async-start(bf16[2,16,2,128,128]{4,1,3,2,0:T(8,128)(2,1)} %broadcast_in_dim.192), calls=%async_computation.1 | async-start | bytes 4194304 | tf_op jit(solution)/shard_map/all_to_all | solution.py:21
  51.5 1.3 copy-start.3
  51.5 1.5 copy-start.2
  51.5 1.6 copy-start.4
  51.5 135.1 %all-gather.2.cloned.1.call-start = ((), (), s32[]{:S(2)}) async-start(), calls=%async_computation.2 | async-start | bytes 8912896 | tf_op jit(solution)/shard_map/all_gather | solution.py:99
  54.9 37.2 %slice-start = ((bf16[2,16,1024,128]{3,2,1,0:T(8,128)(2,1)}), bf16[2,16,128,128]{3,2,1,0:T(8,128)(2,1)S(1)}, s32[]{:S(2)}) async-start(bf16[2,16,1024,128]{3,2,1,0:T(8,128)(2,1)} %param.21), calls=%async_computation.3 | async-start | bytes 2097152 | tf_op jit(solution)/shard_map/slice | solution.py:129
Sparse Core Ops, SparseCore 0:
  54.1 132.4 all-gather.1
where the time goes:
time: 356 us; the launch traced here: 353 us
  matrix products  139 us (39%)
  waiting for transfers between devices  103 us (29%)
  other arithmetic  43.6 us (12%)
  blocking collectives  35.1 us (10%)
  between operations  14.2 us (4%)
  local copies, waits for them, and re-layouts  8.86 us (2%)
  starting transfers between devices  5.93 us (2%)
    all_gather x1, waiting for transfers between devices, on_device(): lax.all_gather(prefix_keyvals, 'ctx', axis=2, tiled=True)  67.1 us
    dot_general x36, matrix products, absorb_step(): jnp.einsum('kgts,skd->kgtd', weights, value_block, preferred_element_type...  67 us
    dot_general x36, matrix products, absorb_step(): jnp.einsum('tkgd,skd->kgts', queries, key_block, preferred_element_type=j...  48.8 us
    all_to_all x1, waiting for transfers between devices, copy_for_each(): return lax.all_to_all(copies, axis, split_axis=0, concat_axis=0, tiled=True)  35.2 us
    all_to_all x1, blocking collectives, copy_for_each(): return lax.all_to_all(copies, axis, split_axis=0, concat_axis=0, tiled=True)  35.1 us
    lt x32, other arithmetic, absorb_step(): allowed = (key_pos < limit)[None, :]  20.9 us
    reduce_sum x45, other arithmetic, refresh(): totals = totals * factor + jnp.sum(weights, axis=-1)  19.4 us
    dot_general x9, matrix products, absorb(): jnp.einsum('rtkgd,rskd->rkgts', decode_heads, key_block, preferred_elemen...  11.8 us
  transfers between devices with their start and end apart: 2, of which 2 were waited for; matrix products, arithmetic and copies ran while one was open for 9% of the time, Pallas kernels for 0%

commit v1 on v0

v1 whole, which is shorter than its diff:
```python
import functools
import math

import jax
import jax.numpy as jnp
from jax import lax
from jax.experimental import pallas as pl
from jax.experimental.pallas import tpu as pltpu
from jax.sharding import PartitionSpec as P

HEAD = 128
GROUP = 8
ROWS = 1024
PREFIX = 1024
PAGE = 128
KEYS = PREFIX + PAGE
NORM_AT = 2 * KEYS
MSG_ROWS = NORM_AT + 16
STATE_ROWS = 144
HALF = 512
SCALE2 = math.log2(math.e) / math.sqrt(HEAD)
EMPTY = -1e30
SAFE = 75.0 * 75.0 * HEAD
Q_OFFSETS = ((0, 0), (2, 0), (0, 3), (2, 3))
K_OFFSETS = ((0, 0), (1, 0), (0, 1), (1, 1))


def xor_pairs(dz, dy):
    return [(z * 4 + y, (z ^ dz) * 4 + (y ^ dy)) for z in range(4) for y in range(4)]


def squares_max(rows):
    ones = jnp.ones((HEAD, HEAD), jnp.bfloat16)
    return jnp.max(jnp.dot(rows * rows, ones, preferred_element_type=jnp.float32))


def prepare_kernel(prefix_ref, stretch_ref, msg_ref):
    msg_ref[:PREFIX] = prefix_ref[0, 0]
    msg_ref[PREFIX:KEYS] = stretch_ref[0, 0]
    for j in range(PREFIX // PAGE):
        msg_ref[KEYS + j * PAGE : KEYS + (j + 1) * PAGE] = prefix_ref[0, 1, j * PAGE : (j + 1) * PAGE].T
    msg_ref[KEYS + PREFIX : NORM_AT] = stretch_ref[0, 1].T
    largest = squares_max(msg_ref[:KEYS]) * 1.02
    msg_ref[NORM_AT:] = jnp.full((16, HEAD), largest, jnp.float32).astype(jnp.bfloat16)


def prepare(prefix, stretch):
    return pl.pallas_call(
        prepare_kernel,
        out_shape=jax.ShapeDtypeStruct((MSG_ROWS, HEAD), jnp.bfloat16),
        compiler_params=pltpu.CompilerParams(vmem_limit_bytes=16 << 20),
        name="prepare",
    )(prefix, stretch)


def effective(state):
    total = jnp.sum(state[128:136], axis=0, keepdims=True)
    return total, jnp.where(total > 0.0, state[136:137], EMPTY)


def combine(first, second):
    total_a, max_a = effective(first)
    total_b, max_b = effective(second)
    top = jnp.maximum(max_a, max_b)
    factor_a, factor_b = jnp.exp2(max_a - top), jnp.exp2(max_b - top)
    summed = first[:128] * factor_a + second[:128] * factor_b
    return summed, total_a * factor_a + total_b * factor_b, top


def fold_kernel(meta, *refs, n_q, n_k, q_at, k_at, prior_at, message):
    q_hbm, refs = refs[:n_q], refs[n_q:]
    k_hbm, refs = refs[:n_k], refs[n_k:]
    if prior_at is not None:
        prior_hbm, refs = refs[0], refs[1:]
    out_ref, qs, ks, vt, norms, state, *rest = refs
    sems = rest[-1]
    copies = []

    def copy(source, target):
        made = pltpu.make_async_copy(source, target, sems.at[len(copies)])
        made.start()
        copies.append(made)

    for i in range(n_q):
        for h in range(GROUP):
            columns = slice(h * HEAD, (h + 1) * HEAD)
            copy(q_hbm[i].at[:, columns], qs.at[i, columns, :])
    for i in range(n_k):
        copy(k_hbm[i].at[pl.ds(0, KEYS)], ks.at[i])
        copy(k_hbm[i].at[pl.ds(NORM_AT, 16)], norms.at[i])
        for j in range(KEYS // PAGE):
            columns = slice(j * PAGE, (j + 1) * PAGE)
            copy(k_hbm[i].at[pl.ds(KEYS + j * PAGE, PAGE)], vt.at[i, :, columns])
    if prior_at is not None:
        prior = rest[0]
        for i in range(n_q):
            copy(prior_hbm.at[prior_at + i], prior.at[i])
    for made in copies:
        made.wait()

    largest_q = functools.reduce(jnp.maximum, [squares_max(qs[i]) for i in range(n_q)]) * 1.02
    largest_k = jnp.max(norms[...].astype(jnp.float32)) * 1.01
    safe = largest_q * largest_k <= SAFE
    limit = meta[0]

    def parts(t, block):
        qi, ki = t // n_k, t % n_k
        q_ctx, k_ctx = meta[4 + q_at + qi], meta[8 + k_at + ki]
        valid = limit - k_ctx * PREFIX

        def prefix_mask(at, rows):
            return lambda: lax.broadcasted_iota(jnp.int32, (rows, ROWS), 0) < valid - at

        def causal_mask():
            token = lax.broadcasted_iota(jnp.int32, (PAGE, ROWS), 1) & (PAGE - 1)
            return k_ctx * PAGE + lax.broadcasted_iota(jnp.int32, (PAGE, ROWS), 0) <= q_ctx * PAGE + token

        @pl.when(valid >= PREFIX)
        def _():
            for at in range(0, PREFIX, HALF):
                block(qi, ki, at, HALF, None)

        @pl.when((valid > 0) & (valid < PREFIX))
        def _():
            for at in range(0, PREFIX, HALF):
                pl.when(valid > at)(functools.partial(block, qi, ki, at, HALF, prefix_mask(at, HALF)))

        @pl.when(k_ctx <= q_ctx)
        def _():
            block(qi, ki, PREFIX, PAGE, causal_mask)

    def scores_of(qi, ki, at, rows):
        keys = ks[ki, at : at + rows, :]
        return lax.dot_general(keys, qs[qi], (((1,), (1,)), ((), ())), preferred_element_type=jnp.float32) * SCALE2

    def fast_block(qi, ki, at, rows, mask):
        weights = jnp.exp2(scores_of(qi, ki, at, rows))
        if mask is not None:
            weights = jnp.where(mask(), weights, 0.0)
        state[qi, 128:136] += jnp.sum(weights.reshape(rows // 8, 8, ROWS), axis=0)
        state[qi, :128] += jnp.dot(
            vt[ki, :, at : at + rows], weights.astype(jnp.bfloat16), preferred_element_type=jnp.float32
        )

    def general_block(qi, ki, at, rows, mask):
        scores = scores_of(qi, ki, at, rows)
        if mask is not None:
            scores = jnp.where(mask(), scores, EMPTY)
        before = state[qi, 136:137]
        top = jnp.maximum(before, jnp.max(scores, axis=0, keepdims=True))
        factor = jnp.exp2(before - top)
        weights = jnp.exp2(scores - top)
        state[qi, 136:144] = jnp.broadcast_to(top, (8, ROWS))
        state[qi, 128:136] = state[qi, 128:136] * factor + jnp.sum(weights.reshape(rows // 8, 8, ROWS), axis=0)
        state[qi, :128] = state[qi, :128] * factor + jnp.dot(
            vt[ki, :, at : at + rows], weights.astype(jnp.bfloat16), preferred_element_type=jnp.float32
        )

    state[:, :136] = jnp.zeros((n_q, 136, ROWS), jnp.float32)

    @pl.when(safe)
    def _():
        state[:, 136:] = jnp.zeros((n_q, 8, ROWS), jnp.float32)
        lax.fori_loop(0, n_q * n_k, lambda t, c: (parts(t, fast_block), c)[1], 0)

    @pl.when(jnp.logical_not(safe))
    def _():
        state[:, 136:] = jnp.full((n_q, 8, ROWS), EMPTY, jnp.float32)
        lax.fori_loop(0, n_q * n_k, lambda t, c: (parts(t, general_block), c)[1], 0)

    for i in range(n_q):
        if prior_at is not None:
            summed, total, top = combine(prior[i], state[i])
        elif message:
            total, top = effective(state[i])
            summed = state[i, :128]
        if message:
            sent = jnp.where(top > EMPTY, 4.0 * jnp.ceil(top * 0.25), EMPTY)
            factor = jnp.exp2(top - sent)
            total = total * factor
            high = total.astype(jnp.bfloat16).astype(jnp.float32)
            row = lax.broadcasted_iota(jnp.int32, (16, ROWS), 0)
            tail = jnp.where(row == 0, high, jnp.where(row == 1, total - high, jnp.where(row == 2, sent, 0.0)))
            out_ref[i, :128] = (summed * factor).astype(jnp.bfloat16)
            out_ref[i, 128:] = tail.astype(jnp.bfloat16)
        elif prior_at is not None:
            row = lax.broadcasted_iota(jnp.int32, (16, ROWS), 0)
            out_ref[i, :128] = summed
            out_ref[i, 128:] = jnp.where(row == 0, total, jnp.where(row < 8, 0.0, top))
        else:
            out_ref[i] = state[i]


def fold(meta, queries, keys, q_at, k_at, prior=None, prior_at=None, message=False, name="fold"):
    n_q, n_k = len(queries), len(keys)
    anywhere = pl.BlockSpec(memory_space=pl.ANY)
    inputs = list(queries) + list(keys) + ([prior] if prior is not None else [])
    scratch = [
        pltpu.VMEM((n_q, ROWS, HEAD), jnp.bfloat16),
        pltpu.VMEM((n_k, KEYS, HEAD), jnp.bfloat16),
        pltpu.VMEM((n_k, HEAD, KEYS), jnp.bfloat16),
        pltpu.VMEM((n_k, 16, HEAD), jnp.bfloat16),
        pltpu.VMEM((n_q, STATE_ROWS, ROWS), jnp.float32),
    ]
    n_copies = 8 * n_q + 11 * n_k
    if prior is not None:
        scratch.append(pltpu.VMEM((n_q, STATE_ROWS, ROWS), jnp.float32))
        n_copies += n_q
    scratch.append(pltpu.SemaphoreType.DMA((n_copies,)))
    work = 4 * n_q * n_k * ROWS * KEYS * HEAD
    return pl.pallas_call(
        functools.partial(
            fold_kernel, n_q=n_q, n_k=n_k, q_at=q_at, k_at=k_at, prior_at=prior_at, message=message
        ),
        out_shape=jax.ShapeDtypeStruct((n_q, STATE_ROWS, ROWS), jnp.bfloat16 if message else jnp.float32),
        in_specs=[pl.BlockSpec(memory_space=pltpu.SMEM)] + [anywhere] * len(inputs),
        scratch_shapes=scratch,
        compiler_params=pltpu.CompilerParams(vmem_limit_bytes=48 << 20),
        cost_estimate=pl.CostEstimate(flops=2 * work, transcendentals=n_q * n_k * ROWS * KEYS, bytes_accessed=n_k * 600000),
        name=name,
    )(meta, *inputs)


def merge_kernel(own_ref, *refs):
    message_refs, out_ref = refs[:-1], refs[-1]
    total, top = effective(own_ref[0])
    tops, totals, sums = [top], [total], [own_ref[0, :128]]
    for ref in message_refs:
        tail = ref[0, 128:].astype(jnp.float32)
        tops.append(tail[2:3])
        totals.append(tail[0:1] + tail[1:2])
        sums.append(ref[0, :128].astype(jnp.float32))
    top = functools.reduce(jnp.maximum, tops)
    factors = [jnp.exp2(t - top) for t in tops]
    total = functools.reduce(jnp.add, [t * f for t, f in zip(totals, factors)])
    inverse = 1.0 / total
    attended = functools.reduce(jnp.add, [s * (f * inverse) for s, f in zip(sums, factors)])
    for h in range(GROUP):
        columns = slice(h * HEAD, (h + 1) * HEAD)
        out_ref[0, :, columns] = attended[:, columns].T.astype(jnp.bfloat16)


def merge(own, messages):
    return pl.pallas_call(
        merge_kernel,
        out_shape=jax.ShapeDtypeStruct((1, PAGE, ROWS), jnp.bfloat16),
        compiler_params=pltpu.CompilerParams(vmem_limit_bytes=16 << 20),
        name="merge",
    )(own, *messages)


def decode_kernel(meta, lengths, q_ref, cache_ref, draft_ref, page_a, page_b, out_ref, *, steps):
    r = pl.program_id(0)
    row_a, row_b, length = meta[1], meta[2], lengths[r]
    queries = q_ref[0]
    rows = queries.shape[0]
    limit = cache_ref.shape[2]

    def with_page(kind):
        block = cache_ref[kind, 0]
        first = jnp.where(r == row_a, page_a[0, kind], jnp.where(r == row_b, page_b[0, kind], block[:PAGE]))
        return jnp.concatenate([first, block[PAGE:]], axis=0)

    def product(keys):
        return lax.dot_general(
            queries, keys, (((1,), (1,)), ((), ())), preferred_element_type=jnp.float32
        ) * SCALE2

    scores = product(with_page(0))
    scores = jnp.where(lax.broadcasted_iota(jnp.int32, (rows, limit), 1) < length, scores, -jnp.inf)
    draft = product(draft_ref[0, 0])
    step = lax.broadcasted_iota(jnp.int32, (rows, steps), 0) // GROUP
    draft = jnp.where(lax.broadcasted_iota(jnp.int32, (rows, steps), 1) <= step, draft, -jnp.inf)
    top = jnp.maximum(jnp.max(scores, axis=1, keepdims=True), jnp.max(draft, axis=1, keepdims=True))
    weights, draft_weights = jnp.exp2(scores - top), jnp.exp2(draft - top)
    total = jnp.sum(weights, axis=1, keepdims=True) + jnp.sum(draft_weights, axis=1, keepdims=True)
    summed = jnp.dot(weights.astype(jnp.bfloat16), with_page(1), preferred_element_type=jnp.float32)
    summed += jnp.dot(draft_weights.astype(jnp.bfloat16), draft_ref[1, 0], preferred_element_type=jnp.float32)
    out_ref[0] = (summed / total).astype(jnp.bfloat16)


def decode(meta, lengths, queries, cache, draft, page_a, page_b):
    row_count, rows, _ = queries.shape
    steps = draft.shape[2]
    limit = cache.shape[2]
    smem = pl.BlockSpec(memory_space=pltpu.SMEM)
    page_spec = pl.BlockSpec((1, 2, PAGE, HEAD), lambda r: (0, 0, 0, 0))
    return pl.pallas_call(
        functools.partial(decode_kernel, steps=steps),
        grid=(row_count,),
        out_shape=jax.ShapeDtypeStruct(queries.shape, jnp.bfloat16),
        in_specs=[
            smem,
            smem,
            pl.BlockSpec((1, rows, HEAD), lambda r: (r, 0, 0)),
            pl.BlockSpec((2, 1, limit, HEAD), lambda r: (0, r, 0, 0)),
            pl.BlockSpec((2, 1, steps, HEAD), lambda r: (0, r, 0, 0)),
            page_spec,
            page_spec,
        ],
        out_specs=pl.BlockSpec((1, rows, HEAD), lambda r: (r, 0, 0)),
        compiler_params=pltpu.CompilerParams(vmem_limit_bytes=16 << 20),
        cost_estimate=pl.CostEstimate(
            flops=32 * row_count * rows * limit * HEAD, transcendentals=row_count * rows * limit, bytes_accessed=8 << 20
        ),
        name="decode",
    )(meta, lengths, queries, cache, draft, page_a, page_b)


def page_targets():
    first, second = [], []
    for n in range(32):
        g, c = n // 16, n % 16
        if n % 4 == 1:
            second.append((n, (n + 1) % 32))
        elif n % 4 == 3:
            first.append((n, g * 16 + (c + 8) % 16))
        else:
            first.append((n, (n + 16) % 32))
    return first, second


def on_device(
    stretch_query,
    prefix_keyvals,
    stretch_key_values,
    stretch_start,
    decode_query,
    draft_key_values,
    decode_cache,
    cache_lengths,
    page_rows,
):
    ctx = lax.axis_index("ctx")
    z, y = ctx // 4, ctx % 4
    block = lax.axis_index(("group", "ctx"))
    row_count, steps, _ = decode_query.shape

    kind = block % 4
    source_a = jnp.where(kind == 3, block - block % 16 + (block + 8) % 16, (block + 16) % 32)
    source_b = jnp.maximum(block - 1, 0)
    row_a = jnp.where(kind == 1, -1, page_rows[source_a] - block * row_count)
    row_b = jnp.where(kind == 2, page_rows[source_b] - block * row_count, -1)
    zero = jnp.zeros((), jnp.int32)
    meta = jnp.stack(
        [stretch_start[0], row_a, row_b, zero]
        + [(z ^ dz) * 4 + (y ^ dy) for dz, dy in Q_OFFSETS]
        + [(z ^ dz) * 4 + (y ^ dy) for dz, dy in K_OFFSETS]
    ).astype(jnp.int32)

    query = stretch_query[0]
    send = lambda x, dz, dy: lax.ppermute(x, "ctx", xor_pairs(dz, dy))
    first, second = page_targets()
    page_a = lax.ppermute(stretch_key_values, ("group", "ctx"), first)
    page_b = lax.ppermute(stretch_key_values, ("group", "ctx"), second)
    query_z = send(query, 2, 0)
    query_y = send(query, 0, 3)
    own = prepare(prefix_keyvals, stretch_key_values)
    keys_z = send(own, 1, 0)
    keys_y = send(own, 0, 1)
    query_d = send(query_z, 0, 3)
    keys_d = send(keys_z, 0, 1)

    decode_rows = decode_query.reshape(row_count, steps * GROUP, HEAD)
    decoded = decode(meta, cache_lengths, decode_rows, decode_cache, draft_key_values, page_a, page_b)
    decode_out = decoded.reshape(decode_query.shape)

    near = fold(meta, [query, query_z, query_y], [own, keys_z, keys_y], 0, 0, name="fold_near")
    message_d = fold(meta, [query_d], [own, keys_z, keys_y, keys_d], 3, 0, message=True, name="fold_far")
    messages = fold(meta, [query_z, query_y], [keys_d], 1, 3, prior=near, prior_at=1, message=True, name="fold_two")
    from_d = send(message_d, 2, 3)
    from_z = send(messages[0:1], 2, 0)
    from_y = send(messages[1:2], 0, 3)
    final = fold(meta, [query], [keys_d], 0, 3, prior=near, prior_at=0, name="fold_own")
    prefill_out = merge(final, [from_d, from_z, from_y])
    return (prefill_out, decode_out)


def solution(mesh):
    return jax.shard_map(
        on_device,
        mesh=mesh,
        in_specs=(
            P("group", "ctx", "tp"),
            P("group", None, "ctx", "tp"),
            P("group", None, "ctx", "tp"),
            P("group"),
            P(("group", "ctx"), None, "tp"),
            P(None, ("group", "ctx"), None, "tp"),
            P(None, ("group", "ctx"), None, "tp"),
            P(("group", "ctx")),
            P(),
        ),
        out_specs=(P("group", "ctx", "tp"), P(("group", "ctx"), None, "tp")),
        check_vma=False,
    )
```

time: 356 us -> 95.6 us (0.27)
  the two profiles are of different devices: /device:TPU:2 before, /device:TPU:228 now
where the time goes in v1:
time: 95.6 us; the launch traced here: 95.7 us
  Pallas kernels  54.9 us (57%)
  starting transfers between devices  23 us (24%)
  waiting for transfers between devices  7.5 us (8%)
  local copies, waits for them, and re-layouts  7.41 us (8%)
  between operations  2.86 us (3%)
    pallas_call x4, Pallas kernels, fold(): pl.pallas_call(functools.partial(fold_kernel, n_q=n_q, n_k=n_k, q_at=q_at...  44.1 us
    ppermute x9, starting transfers between devices, on_device(): send = lambda x, dz, dy: lax.ppermute(x, 'ctx', xor_pairs(dz, dy))  19.6 us
    pallas_call x1, Pallas kernels, decode(): pl.pallas_call(functools.partial(decode_kernel, steps=steps), grid=(row_c...  8.59 us
    ppermute x9, waiting for transfers between devices, on_device(): send = lambda x, dz, dy: lax.ppermute(x, 'ctx', xor_pairs(dz, dy))  7.5 us
    unnamed x18, local copies, waits for them, and re-layouts  3.49 us
    ppermute x1, starting transfers between devices, on_device(): page_a = lax.ppermute(stretch_key_values, ('group', 'ctx'), first)  2.71 us
  transfers between devices with their start and end apart: 11, of which 2 were waited for; matrix products, arithmetic and copies ran while one was open for 4% of the time, Pallas kernels for 55%

profile of v1, /device:TPU:228, one launch (start us, length us, event | category | flops | bytes accessed | tf_op | source)
XLA Modules:
  0.0 95.7 jit_solution(17175663551981655136)
XLA Ops:
  0.6 1.0 %copy-done = bf16[1,2,1024,128]{3,2,1,0:T(8,128)(2,1)S(1)} copy-done((bf16[1,2,1024,128]{3,2,1,0:T(8,128)(2,1)S(1)}, bf16[1,2,1024,128]{3,2,1,0:T(8,128)(2,1)}, u32[]{:S(2)}) %copy-start) | copy-done | bytes 524312
  1.7 1.2 %prepare.1.refs_3_.refs_1_ = bf16[2320,128]{1,0:T(8,128)(2,1)S(1)} custom-call(bf16[1,2,1024,128]{3,2,1,0:T(8,128)(2,1)S(1)} %copy-done, bf16[1,2,128,128]{3,2,1,0:T(8,128)(2,1)} %stretch_ref.1), custom_call_target="tpu_custom_call" | custom-call | tf_op jit(solution)/shard_map/prepare/pallas_call | solution.py:48
  2.9 1.1 %collective-permute-start = (bf16[2320,128]{1,0:T(8,128)(2,1)S(1)}, bf16[2320,128]{1,0:T(8,128)(2,1)S(1)}, u32[]{:S(2)}, u32[]{:S(2)}) collective-permute-start(bf16[2320,128]{1,0:T(8,128)(2,1)S(1)} %prepare.1.refs_3_.refs_1_), channel_id=1, source_target_pairs={{0,32},{8,40},{16,48},{24,56},{32,0},{40,8},{48,16},{56,24},{64,96... | collective-permute-start | bytes 1781768 | tf_op jit(solution)/shard_map/ppermute | solution.py:352
  4.0 1.6 %collective-permute-start.4 = (bf16[2320,128]{1,0:T(8,128)(2,1)S(1)}, bf16[2320,128]{1,0:T(8,128)(2,1)S(1)}, u32[]{:S(2)}, u32[]{:S(2)}) collective-permute-start(bf16[2320,128]{1,0:T(8,128)(2,1)S(1)} %prepare.1.refs_3_.refs_1_), channel_id=1, source_target_pairs={{0,8},{8,0},{16,24},{24,16},{32,40},{40,32},{48,56},{56,48},{64,72... | collective-permute-start | bytes 1781768 | tf_op jit(solution)/shard_map/ppermute | solution.py:352
  5.6 2.2 %collective-permute-start.3 = (bf16[128,1024]{1,0:T(8,128)(2,1)}, bf16[128,1024]{1,0:T(8,128)(2,1)S(1)}, u32[]{:S(2)}, u32[]{:S(2)}) collective-permute-start(bf16[128,1024]{1,0:T(8,128)(2,1)} %bitcast.14), channel_id=1, source_target_pairs={{0,24},{8,16},{16,8},{24,0},{32,56},{40,48},{48,40},{56,32},{64,88... | collective-permute-start | bytes 786440 | tf_op jit(solution)/shard_map/ppermute | solution.py:352
  7.7 1.5 %collective-permute-start.2 = (bf16[128,1024]{1,0:T(8,128)(2,1)}, bf16[128,1024]{1,0:T(8,128)(2,1)S(1)}, u32[]{:S(2)}, u32[]{:S(2)}) collective-permute-start(bf16[128,1024]{1,0:T(8,128)(2,1)} %bitcast.15), channel_id=1, source_target_pairs={{0,64},{8,72},{16,80},{24,88},{32,96},{40,104},{48,112},{56,120},{... | collective-permute-start | bytes 786440 | tf_op jit(solution)/shard_map/ppermute | solution.py:352
  9.2 0.7 collective-permute-start.10
  10.6 1.3 %fusion.1 = (s32[1]{0:T(128)}, s32[1]{0:T(128)}) fusion(s32[32]{0:T(128)} %param.17, s32[]{:T(128)S(6)} %max.3, s32[]{:T(128)S(6)} %select_n.47), kind=kLoop, calls=%fused_computation.1 | loop fusion | bytes 24 | tf_op jit(solution)/shard_map/dynamic_slice | solution.py:343
  13.2 1.0 %reshape.10.q_ref = bf16[16,32,128]{2,1,0:T(8,128)(2,1)S(1)} reshape(bf16[16,4,1024]{2,1,0:T(4,128)(2,1)} %param.13) | data formatting | bytes 262144 | tf_op jit(solution)/shard_map/reshape | solution.py:364
  14.2 0.1 stack.40.meta
  14.3 0.2 collective-permute-done.3.refs_2_.refs_1_
  14.5 2.7 %collective-permute-start.9 = (bf16[1,2,128,128]{3,2,1,0:T(8,128)(2,1)}, bf16[1,2,128,128]{3,2,1,0:T(8,128)(2,1)S(1)}, u32[]{:S(2)}, u32[]{:S(2)}) collective-permute-start(bf16[1,2,128,128]{3,2,1,0:T(8,128)(2,1)} %stretch_ref.1), channel_id=1, source_target_pairs={{0,128},{16,144},{24,88},{32,160},{48,176},{56,120},{64,192},{80,2... | collective-permute-start | bytes 196616 | tf_op jit(solution)/shard_map/ppermute | solution.py:354
  17.2 7.3 %collective-permute-done.2.refs_1_.refs_0_ = bf16[128,1024]{1,0:T(8,128)(2,1)S(1)} collective-permute-done((bf16[128,1024]{1,0:T(8,128)(2,1)}, bf16[128,1024]{1,0:T(8,128)(2,1)S(1)}, u32[]{:S(2)}, u32[]{:S(2)}) %collective-permute-start.2) | collective-permute-done | bytes 262176 | tf_op jit(solution)/shard_map/ppermute | solution.py:352
  24.5 1.7 %collective-permute-start.5 = (bf16[128,1024]{1,0:T(8,128)(2,1)S(1)}, bf16[128,1024]{1,0:T(8,128)(2,1)S(1)}, u32[]{:S(2)}, u32[]{:S(2)}) collective-permute-start(bf16[128,1024]{1,0:T(8,128)(2,1)S(1)} %collective-permute-done.2.refs_1_.refs_0_), channel_id=1, source_target_pairs={{0,24},{8,16},{16,8},{24,0},{32,56},{40,48},{48,40},{56,32},{64,88... | collective-permute-start | bytes 786440 | tf_op jit(solution)/shard_map/ppermute | solution.py:352
  26.1 1.5 %collective-permute-start.1 = (bf16[2320,128]{1,0:T(8,128)(2,1)S(1)}, bf16[2320,128]{1,0:T(8,128)(2,1)S(1)}, u32[]{:S(2)}, u32[]{:S(2)}) collective-permute-start(bf16[2320,128]{1,0:T(8,128)(2,1)S(1)} %collective-permute-done.refs_4_.refs_2_), channel_id=1, source_target_pairs={{0,8},{8,0},{16,24},{24,16},{32,40},{40,32},{48,56},{56,48},{64,72... | collective-permute-start | bytes 1781768 | tf_op jit(solution)/shard_map/ppermute | solution.py:352
  27.6 0.0 collective-permute-done.4.refs_5_.refs_3_
  27.6 0.9 copy-done.3
  28.6 23.2 %fold_near.1.refs_2_.refs_3_ = f32[3,144,1024]{2,1,0:T(8,128)S(1)} custom-call(s32[12]{0:T(128)S(1)} %stack.40.meta, bf16[128,1024]{1,0:T(8,128)(2,1)S(1)} %bitcast.16, bf16[128,1024]{1,0:T(8,128)(2,1)S(1)} %collective-permute-done.2.refs_1_.refs_0_, bf16[128,1024]{1,0:T(8,128)(2,1)S(1)} %collective-permute-done.3.refs_2_.refs_1_, ...), custom_call_target="tpu_custom_call" | custom-call | flops 10871635968 | bytes 1800000 | tf_op jit(solution)/shard_map/fold_near/pallas_call | solution.py:211
  51.8 0.0 collective-permute-done.1.refs_1_.refs_4_.refs_2_
  51.8 6.6 %fold_two.1 = bf16[2,144,1024]{2,1,0:T(8,128)(2,1)S(1)} custom-call(s32[12]{0:T(128)S(1)} %stack.40.meta, bf16[128,1024]{1,0:T(8,128)(2,1)S(1)} %collective-permute-done.2.refs_1_.refs_0_, bf16[128,1024]{1,0:T(8,128)(2,1)S(1)} %collective-permute-done.3.refs_2_.refs_1_, bf16[2320,128]{1,0:T(8,128)(2,1)S(1)} %collective-permute-done.1.refs_1_.refs_4_.refs_2_, ...), custom_call_target="tpu_custom_call" | custom-call | flops 2415919104 | bytes 600000 | tf_op jit(solution)/shard_map/fold_two/pallas_call | solution.py:211
  58.4 0.9 fusion
  59.2 1.9 %collective-permute-start.8 = (bf16[1,144,1024]{2,1,0:T(8,128)(2,1)}, bf16[1,144,1024]{2,1,0:T(8,128)(2,1)S(1)}, u32[]{:S(2)}, u32[]{:S(2)}) collective-permute-start(bf16[1,144,1024]{2,1,0:T(8,128)(2,1)} %get-tuple-element.2), channel_id=1, source_target_pairs={{0,24},{8,16},{16,8},{24,0},{32,56},{40,48},{48,40},{56,32},{64,88... | collective-permute-start | bytes 884744 | tf_op jit(solution)/shard_map/ppermute | solution.py:352
  61.1 3.6 %collective-permute-start.7 = (bf16[1,144,1024]{2,1,0:T(8,128)(2,1)}, bf16[1,144,1024]{2,1,0:T(8,128)(2,1)S(1)}, u32[]{:S(2)}, u32[]{:S(2)}) collective-permute-start(bf16[1,144,1024]{2,1,0:T(8,128)(2,1)} %get-tuple-element.3), channel_id=1, source_target_pairs={{0,64},{8,72},{16,80},{24,88},{32,96},{40,104},{48,112},{56,120},{... | collective-permute-start | bytes 884744 | tf_op jit(solution)/shard_map/ppermute | solution.py:352
  64.7 10.3 %fold_far.1 = bf16[1,144,1024]{2,1,0:T(8,128)(2,1)S(1)} custom-call(s32[12]{0:T(128)S(1)} %stack.40.meta, bf16[128,1024]{1,0:T(8,128)(2,1)S(1)} %collective-permute-done.5.refs_0_, bf16[2320,128]{1,0:T(8,128)(2,1)S(1)} %prepare.1.refs_3_.refs_1_, bf16[2320,128]{1,0:T(8,128)(2,1)S(1)} %collective-permute-done.refs_4_.refs_2_, ...), custom_call_target="tpu_custom_call" | custom-call | flops 4831838208 | bytes 2400000 | tf_op jit(solution)/shard_map/fold_far/pallas_call | solution.py:211
  75.1 0.0 copy-start.4
  75.1 4.7 %collective-permute-start.6 = (bf16[1,144,1024]{2,1,0:T(8,128)(2,1)S(1)}, bf16[1,144,1024]{2,1,0:T(8,128)(2,1)S(1)}, u32[]{:S(2)}, u32[]{:S(2)}) collective-permute-start(bf16[1,144,1024]{2,1,0:T(8,128)(2,1)S(1)} %fold_far.1), channel_id=1, source_target_pairs={{0,88},{8,80},{16,72},{24,64},{32,120},{40,112},{48,104},{56,96},{... | collective-permute-start | bytes 884744 | tf_op jit(solution)/shard_map/ppermute | solution.py:352
  79.8 8.6 %decode.1 = bf16[16,32,128]{2,1,0:T(8,128)(2,1)S(1)} custom-call(s32[12]{0:T(128)S(1)} %stack.40.meta, s32[16]{0:T(128)S(1)} %copy-done.2, bf16[16,32,128]{2,1,0:T(8,128)(2,1)S(1)} %reshape.10.q_ref, bf16[2,16,1024,128]{3,2,1,0:T(8,128)(2,1)S(1)} %bitcast.13, bf16[2,16,4,128]{3,2,1,0:T(4,128)(2,1)S(1)} %copy-done.1, ...), custom_call_target="tpu_custom_call" | custom-call | flops 2147483648 | bytes 8388608 | tf_op jit(solution)/shard_map/decode/pallas_call | solution.py:288
  88.4 0.7 reshape.11
  89.1 1.5 %copy-done.6 = f32[3,144,1024]{2,1,0:T(8,128)S(1)} copy-done((f32[3,144,1024]{2,1,0:T(8,128)S(1)}, f32[3,144,1024]{2,1,0:T(8,128)}, u32[]{:S(2)}) %copy-start.6) | copy-done | bytes 1769496
  90.6 4.0 %fold_own.1.own_ref = f32[1,144,1024]{2,1,0:T(8,128)S(1)} custom-call(s32[12]{0:T(128)S(1)} %stack.40.meta, bf16[128,1024]{1,0:T(8,128)(2,1)S(1)} %bitcast.17, bf16[2320,128]{1,0:T(8,128)(2,1)S(1)} %collective-permute-done.1.refs_1_.refs_4_.refs_2_, f32[3,144,1024]{2,1,0:T(8,128)S(1)} %copy-done.6), custom_call_target="tpu_custom_call" | custom-call | flops 1207959552 | bytes 600000 | tf_op jit(solution)/shard_map/fold_own/pallas_call | solution.py:211
  94.6 0.0 collective-permute-done.8.refs_2_
  94.6 1.0 %merge.1 = bf16[1,128,1024]{2,1,0:T(8,128)(2,1)} custom-call(f32[1,144,1024]{2,1,0:T(8,128)S(1)} %fold_own.1.own_ref, bf16[1,144,1024]{2,1,0:T(8,128)(2,1)S(1)} %collective-permute-done.6.refs_0_, bf16[1,144,1024]{2,1,0:T(8,128)(2,1)S(1)} %collective-permute-done.7.refs_1_, bf16[1,144,1024]{2,1,0:T(8,128)(2,1)S(1)} %collective-permute-done.8.refs_2_), custom_call_target="tpu_custom_call" | custom-call | tf_op jit(solution)/shard_map/merge/pallas_call | solution.py:244
  (21 shorter events, 0.0 us)
Async XLA Ops:
  0.6 1.0 %copy-start = (bf16[1,2,1024,128]{3,2,1,0:T(8,128)(2,1)S(1)}, bf16[1,2,1024,128]{3,2,1,0:T(8,128)(2,1)}, u32[]{:S(2)}) copy-start(bf16[1,2,1024,128]{3,2,1,0:T(8,128)(2,1)} %prefix_ref.1) | copy-start | bytes 1572868
  2.9 23.3 %collective-permute-start = (bf16[2320,128]{1,0:T(8,128)(2,1)S(1)}, bf16[2320,128]{1,0:T(8,128)(2,1)S(1)}, u32[]{:S(2)}, u32[]{:S(2)}) collective-permute-start(bf16[2320,128]{1,0:T(8,128)(2,1)S(1)} %prepare.1.refs_3_.refs_1_), channel_id=1, source_target_pairs={{0,32},{8,40},{16,48},{24,56},{32,0},{40,8},{48,16},{56,24},{64,96... | collective-permute-start | bytes 1781768 | tf_op jit(solution)/shard_map/ppermute | solution.py:352
  4.0 23.7 %collective-permute-start.4 = (bf16[2320,128]{1,0:T(8,128)(2,1)S(1)}, bf16[2320,128]{1,0:T(8,128)(2,1)S(1)}, u32[]{:S(2)}, u32[]{:S(2)}) collective-permute-start(bf16[2320,128]{1,0:T(8,128)(2,1)S(1)} %prepare.1.refs_3_.refs_1_), channel_id=1, source_target_pairs={{0,8},{8,0},{16,24},{24,16},{32,40},{40,32},{48,56},{56,48},{64,72... | collective-permute-start | bytes 1781768 | tf_op jit(solution)/shard_map/ppermute | solution.py:352
  5.6 8.9 %collective-permute-start.3 = (bf16[128,1024]{1,0:T(8,128)(2,1)}, bf16[128,1024]{1,0:T(8,128)(2,1)S(1)}, u32[]{:S(2)}, u32[]{:S(2)}) collective-permute-start(bf16[128,1024]{1,0:T(8,128)(2,1)} %bitcast.14), channel_id=1, source_target_pairs={{0,24},{8,16},{16,8},{24,0},{32,56},{40,48},{48,40},{56,32},{64,88... | collective-permute-start | bytes 786440 | tf_op jit(solution)/shard_map/ppermute | solution.py:352
  7.7 16.7 %collective-permute-start.2 = (bf16[128,1024]{1,0:T(8,128)(2,1)}, bf16[128,1024]{1,0:T(8,128)(2,1)S(1)}, u32[]{:S(2)}, u32[]{:S(2)}) collective-permute-start(bf16[128,1024]{1,0:T(8,128)(2,1)} %bitcast.15), channel_id=1, source_target_pairs={{0,64},{8,72},{16,80},{24,88},{32,96},{40,104},{48,112},{56,120},{... | collective-permute-start | bytes 786440 | tf_op jit(solution)/shard_map/ppermute | solution.py:352
  9.2 70.6 %collective-permute-start.10 = (bf16[1,2,128,128]{3,2,1,0:T(8,128)(2,1)}, bf16[1,2,128,128]{3,2,1,0:T(8,128)(2,1)S(1)}, u32[]{:S(2)}, u32[]{:S(2)}) collective-permute-start(bf16[1,2,128,128]{3,2,1,0:T(8,128)(2,1)} %stretch_ref.1), channel_id=1, source_target_pairs={{8,16},{40,48},{72,80},{104,112},{136,144},{168,176},{200,208},{23... | collective-permute-start | bytes 196616 | tf_op jit(solution)/shard_map/ppermute | solution.py:355
  14.5 65.3 %collective-permute-start.9 = (bf16[1,2,128,128]{3,2,1,0:T(8,128)(2,1)}, bf16[1,2,128,128]{3,2,1,0:T(8,128)(2,1)S(1)}, u32[]{:S(2)}, u32[]{:S(2)}) collective-permute-start(bf16[1,2,128,128]{3,2,1,0:T(8,128)(2,1)} %stretch_ref.1), channel_id=1, source_target_pairs={{0,128},{16,144},{24,88},{32,160},{48,176},{56,120},{64,192},{80,2... | collective-permute-start | bytes 196616 | tf_op jit(solution)/shard_map/ppermute | solution.py:354
  24.5 40.2 %collective-permute-start.5 = (bf16[128,1024]{1,0:T(8,128)(2,1)S(1)}, bf16[128,1024]{1,0:T(8,128)(2,1)S(1)}, u32[]{:S(2)}, u32[]{:S(2)}) collective-permute-start(bf16[128,1024]{1,0:T(8,128)(2,1)S(1)} %collective-permute-done.2.refs_1_.refs_0_), channel_id=1, source_target_pairs={{0,24},{8,16},{16,8},{24,0},{32,56},{40,48},{48,40},{56,32},{64,88... | collective-permute-start | bytes 786440 | tf_op jit(solution)/shard_map/ppermute | solution.py:352
  26.1 25.6 %collective-permute-start.1 = (bf16[2320,128]{1,0:T(8,128)(2,1)S(1)}, bf16[2320,128]{1,0:T(8,128)(2,1)S(1)}, u32[]{:S(2)}, u32[]{:S(2)}) collective-permute-start(bf16[2320,128]{1,0:T(8,128)(2,1)S(1)} %collective-permute-done.refs_4_.refs_2_), channel_id=1, source_target_pairs={{0,8},{8,0},{16,24},{24,16},{32,40},{40,32},{48,56},{56,48},{64,72... | collective-permute-start | bytes 1781768 | tf_op jit(solution)/shard_map/ppermute | solution.py:352
  27.6 1.0 copy-start.3
  51.8 23.3 %copy-start.5 = (f32[3,144,1024]{2,1,0:T(8,128)}, f32[3,144,1024]{2,1,0:T(8,128)S(1)}, u32[]{:S(2)}) copy-start(f32[3,144,1024]{2,1,0:T(8,128)S(1)} %fold_near.1.refs_2_.refs_3_) | copy-start | bytes 5308420
  59.2 35.4 %collective-permute-start.8 = (bf16[1,144,1024]{2,1,0:T(8,128)(2,1)}, bf16[1,144,1024]{2,1,0:T(8,128)(2,1)S(1)}, u32[]{:S(2)}, u32[]{:S(2)}) collective-permute-start(bf16[1,144,1024]{2,1,0:T(8,128)(2,1)} %get-tuple-element.2), channel_id=1, source_target_pairs={{0,24},{8,16},{16,8},{24,0},{32,56},{40,48},{48,40},{56,32},{64,88... | collective-permute-start | bytes 884744 | tf_op jit(solution)/shard_map/ppermute | solution.py:352
  61.1 18.6 %slice-start = ((s8[8388608]{0:T(1024)(128)(4,1)}), s8[4194304]{0:T(1024)(128)(4,1)S(1)}, s32[]{:S(2)}) async-start(s8[8388608]{0:T(1024)(128)(4,1)} %bitcast.12), calls=%async_computation | async-start | bytes 8388608
  61.1 18.6 %slice-start.1 = ((s8[8388608]{0:T(1024)(128)(4,1)}), s8[4194304]{0:T(1024)(128)(4,1)S(1)}, s32[]{:S(2)}) async-start(s8[8388608]{0:T(1024)(128)(4,1)} %bitcast.12), calls=%async_computation.1 | async-start | bytes 8388608
  61.1 18.6 %copy-start.1 = (bf16[2,16,4,128]{3,2,1,0:T(4,128)(2,1)S(1)}, bf16[2,16,4,128]{3,2,1,0:T(4,128)(2,1)}, u32[]{:S(2)}) copy-start(bf16[2,16,4,128]{3,2,1,0:T(4,128)(2,1)} %draft_ref.1) | copy-start | bytes 98308
  61.1 18.7 %copy-start.2 = (s32[16]{0:T(128)S(1)}, s32[16]{0:T(128)}, u32[]{:S(2)}) copy-start(s32[16]{0:T(128)} %lengths.1) | copy-start | bytes 196
  61.1 33.5 %collective-permute-start.7 = (bf16[1,144,1024]{2,1,0:T(8,128)(2,1)}, bf16[1,144,1024]{2,1,0:T(8,128)(2,1)S(1)}, u32[]{:S(2)}, u32[]{:S(2)}) collective-permute-start(bf16[1,144,1024]{2,1,0:T(8,128)(2,1)} %get-tuple-element.3), channel_id=1, source_target_pairs={{0,64},{8,72},{16,80},{24,88},{32,96},{40,104},{48,112},{56,120},{... | collective-permute-start | bytes 884744 | tf_op jit(solution)/shard_map/ppermute | solution.py:352
  75.1 14.0 %copy-start.4 = (bf16[1,128,1024]{2,1,0:T(8,128)(2,1)S(1)}, bf16[1,128,1024]{2,1,0:T(8,128)(2,1)}, u32[]{:S(2)}) copy-start(bf16[1,128,1024]{2,1,0:T(8,128)(2,1)} %param.9) | copy-start | bytes 786436
  75.1 19.6 %collective-permute-start.6 = (bf16[1,144,1024]{2,1,0:T(8,128)(2,1)S(1)}, bf16[1,144,1024]{2,1,0:T(8,128)(2,1)S(1)}, u32[]{:S(2)}, u32[]{:S(2)}) collective-permute-start(bf16[1,144,1024]{2,1,0:T(8,128)(2,1)S(1)} %fold_far.1), channel_id=1, source_target_pairs={{0,88},{8,80},{16,72},{24,64},{32,120},{40,112},{48,104},{56,96},{... | collective-permute-start | bytes 884744 | tf_op jit(solution)/shard_map/ppermute | solution.py:352
  89.1 1.5 %copy-start.6 = (f32[3,144,1024]{2,1,0:T(8,128)S(1)}, f32[3,144,1024]{2,1,0:T(8,128)}, u32[]{:S(2)}) copy-start(f32[3,144,1024]{2,1,0:T(8,128)} %copy-done.5) | copy-start | bytes 5308420

commit v2 on v0

v2 whole, which is shorter than its diff:
```python
import functools
import math

import jax
import jax.numpy as jnp
from jax import lax
from jax.experimental import pallas as pl
from jax.experimental.pallas import tpu as pltpu
from jax.sharding import PartitionSpec as P

HEAD = 128
GROUP = 8
ROWS = 1024
PREFIX = 1024
PAGE = 128
KEYS = PREFIX + PAGE
HALF = 512
NORM_AT = 2 * HALF
STRETCH_AT = NORM_AT + 16
FIRST_ROWS = STRETCH_AT + 2 * PAGE
SECOND_ROWS = STRETCH_AT
QUERY_ROWS = ROWS + 16
STATE_ROWS = 144
SCALE2 = math.log2(math.e) / math.sqrt(HEAD)
EMPTY = -1e30
SAFE = 75.0 * 75.0 * HEAD
Q_OFFSETS = ((0, 0), (1, 3), (1, 0), (0, 3))
K_OFFSETS = ((0, 0), (0, 1), (2, 0), (2, 1))


def xor_pairs(dz, dy):
    return [(z * 4 + y, (z ^ dz) * 4 + (y ^ dy)) for z in range(4) for y in range(4)]


def block_of(ctx, dz, dy):
    z, y = ctx // 4, ctx % 4
    flip = {0: lambda v: v, 1: lambda v: v + 1 - 2 * (v % 2), 2: lambda v: (v + 2) % 4, 3: lambda v: 3 - v}
    return flip[dz](z) * 4 + flip[dy](y)


def squares_max(rows):
    ones = jnp.ones((HEAD, HEAD), jnp.bfloat16)
    return jnp.max(jnp.dot(rows * rows, ones, preferred_element_type=jnp.float32))


def norm_rows(rows):
    return jnp.full((16, HEAD), squares_max(rows) * 1.04, jnp.float32).astype(jnp.bfloat16)


def prepare_kernel(query_hbm, prefix_hbm, stretch_hbm, query_msg, whole, first, second, keys, values, sems):
    copies = [
        (query_hbm.at[0, :, h * HEAD : (h + 1) * HEAD], query_msg.at[h * HEAD : (h + 1) * HEAD]) for h in range(GROUP)
    ]
    copies += [
        (prefix_hbm.at[0, 0], keys.at[:PREFIX]),
        (stretch_hbm.at[0, 0], keys.at[PREFIX:]),
        (prefix_hbm.at[0, 1], values.at[:PREFIX]),
        (stretch_hbm.at[0, 1], values.at[PREFIX:]),
    ]
    copies = [pltpu.make_async_copy(a, b, sems.at[i]) for i, (a, b) in enumerate(copies)]
    for made in copies:
        made.start()
    for made in copies[GROUP:]:
        made.wait()
    norms = norm_rows(keys[...])
    for at, part, base in ((0, first, 0), (HALF, second, FIRST_ROWS)):
        pieces = [(0, keys[at : at + HALF]), (NORM_AT, norms)]
        pieces += [(HALF + j, values[at + j : at + j + PAGE].T) for j in range(0, HALF, PAGE)]
        if base == 0:
            pieces += [(STRETCH_AT, keys[PREFIX:]), (STRETCH_AT + PAGE, values[PREFIX:].T)]
        for row, piece in pieces:
            part[row : row + piece.shape[0]] = piece
            whole[base + row : base + row + piece.shape[0]] = piece
    for made in copies[:GROUP]:
        made.wait()
    query_msg[ROWS:] = norm_rows(query_msg[:ROWS])


def prepare(query, prefix, stretch):
    in_hbm = [pltpu.with_memory_space_constraint(x, pltpu.HBM) for x in (query, prefix, stretch)]
    return pl.pallas_call(
        prepare_kernel,
        out_shape=[
            jax.ShapeDtypeStruct((rows, HEAD), jnp.bfloat16)
            for rows in (QUERY_ROWS, FIRST_ROWS + SECOND_ROWS, FIRST_ROWS, SECOND_ROWS)
        ],
        in_specs=[pl.BlockSpec(memory_space=pl.ANY)] * 3,
        scratch_shapes=[
            pltpu.VMEM((KEYS, HEAD), jnp.bfloat16),
            pltpu.VMEM((KEYS, HEAD), jnp.bfloat16),
            pltpu.SemaphoreType.DMA((GROUP + 4,)),
        ],
        compiler_params=pltpu.CompilerParams(vmem_limit_bytes=16 << 20),
        name="prepare",
    )(*in_hbm)


def effective(state):
    total = jnp.sum(state[128:136], axis=0, keepdims=True)
    return total, jnp.where(total > 0.0, state[136:137], EMPTY)


def fold_kernel(start, *refs, n_q, q_at, n_in, parts, has_prior, message):
    n_h = len(parts)
    q_in, refs = refs[:n_q], refs[n_q:]
    k_in, refs = refs[:n_in], refs[n_in:]
    prior_in, refs = (refs[:n_q], refs[n_q:]) if has_prior else ((), refs)
    outs, refs = refs[:n_q], refs[n_q:]
    qs, ks, state, table, stretch_table, sems = refs
    pairs = [(q_in[i], qs.at[i]) for i in range(n_q)]
    for i, (source, row, _, half) in enumerate(parts):
        rows = SECOND_ROWS if half else FIRST_ROWS
        pairs.append((k_in[source].at[pl.ds(row, rows)], ks.at[i, pl.ds(0, rows)]))
    pairs += [(prior_in[i], state.at[i]) for i in range(len(prior_in))]
    copies = [pltpu.make_async_copy(a, b, sems.at[i]) for i, (a, b) in enumerate(pairs)]
    for made in copies:
        made.start()
    limit = start[0]
    ctx = lax.axis_index("ctx")
    k_ctx = [block_of(ctx, *offset) for offset in K_OFFSETS]
    q_ctx = [block_of(ctx, *offset) for offset in Q_OFFSETS]
    valid = [limit - k_ctx[slot] * PREFIX - half * HALF for _, _, slot, half in parts]
    count, edge, edge_valid = jnp.int32(0), jnp.int32(0), jnp.int32(0)
    for qi in range(n_q):
        for hi in range(n_h):
            table[count] = qi * n_h + hi
            count += (valid[hi] >= HALF).astype(jnp.int32)
    for hi in range(n_h):
        cut = (valid[hi] > 0) & (valid[hi] < HALF)
        edge, edge_valid = jnp.where(cut, hi, edge), jnp.where(cut, valid[hi], edge_valid)
    with_stretch = [(hi, slot) for hi, (_, _, slot, half) in enumerate(parts) if half == 0]
    stretches = jnp.int32(0)
    for qi in range(n_q):
        for hi, slot in with_stretch:
            apart = q_ctx[q_at + qi] - k_ctx[slot]
            stretch_table[stretches] = qi + 4 * hi + 64 * jnp.maximum(apart, 0)
            stretches += (apart >= 0).astype(jnp.int32)
    for made in copies:
        made.wait()
    largest_q = jnp.max(qs[:, ROWS:].astype(jnp.float32))
    largest_k = jnp.max(ks[:, NORM_AT:STRETCH_AT].astype(jnp.float32))
    safe = largest_q * largest_k <= SAFE
    if has_prior:
        safe &= jnp.max(jnp.abs(state[:, 136:])) == 0.0

    def raw_scores(qi, keys):
        return lax.dot_general(keys, qs[qi, :ROWS], (((1,), (1,)), ((), ())), preferred_element_type=jnp.float32)

    def values_of(hi):
        return jnp.concatenate([ks[hi, HALF + j : HALF + j + PAGE] for j in range(0, HALF, PAGE)], axis=1)

    def sublane_sums(weights):
        return jnp.sum(weights.reshape(weights.shape[0] // 8, 8, ROWS), axis=0)

    def fast_add(qi, raw, values, mask=None):
        weights = jnp.exp2(raw * SCALE2)
        if mask is not None:
            weights = jnp.where(mask, weights, 0.0)
        state[qi, 128:136] += sublane_sums(weights)
        state[qi, :128] += jnp.dot(values, weights.astype(jnp.bfloat16), preferred_element_type=jnp.float32)

    def key_minus_token():
        token = lax.broadcasted_iota(jnp.int32, (PAGE, ROWS), 1) & (PAGE - 1)
        return lax.broadcasted_iota(jnp.int32, (PAGE, ROWS), 0) - token

    def query_block(qi):
        block = q_ctx[q_at]
        for i in range(1, n_q):
            block = jnp.where(qi == i, q_ctx[q_at + i], block)
        return block

    def fold_stretch(t, c):
        task = stretch_table[t]
        qi, hi, apart = task % 4, task // 4 % 16, task // 64
        keys, values = ks[hi, STRETCH_AT : STRETCH_AT + PAGE], ks[hi, STRETCH_AT + PAGE : FIRST_ROWS]
        fast_add(qi, raw_scores(qi, keys), values, key_minus_token() <= apart * PAGE)
        return c

    def fold_edge(qi, c):
        mask = lax.broadcasted_iota(jnp.int32, (HALF, ROWS), 0) < edge_valid
        fast_add(qi, raw_scores(qi, ks[edge, :HALF]), values_of(edge), mask)
        return c

    def general_add(qi, keys, values, mask):
        scores = jnp.where(mask, raw_scores(qi, keys) * SCALE2, EMPTY)
        before = state[qi, 136:137]
        top = jnp.maximum(before, jnp.max(scores, axis=0, keepdims=True))
        factor = jnp.exp2(before - top)
        weights = jnp.where(mask, jnp.exp2(scores - top), 0.0)
        state[qi, 136:144] = jnp.broadcast_to(top, (8, ROWS))
        state[qi, 128:136] = state[qi, 128:136] * factor + sublane_sums(weights)
        state[qi, :128] = state[qi, :128] * factor + jnp.dot(
            values, weights.astype(jnp.bfloat16), preferred_element_type=jnp.float32
        )

    def general_part(hi, slot, half):
        def one(t, c):
            qi, j = t // 4, t % 4
            at = pl.multiple_of(j * PAGE, PAGE)
            keys = limit - k_ctx[slot] * PREFIX - half * HALF - at
            mask = lax.broadcasted_iota(jnp.int32, (PAGE, ROWS), 0) < keys
            general_add(qi, ks[hi, pl.ds(at, PAGE)], ks[hi, pl.ds(pl.multiple_of(HALF + at, PAGE), PAGE)], mask)
            return c

        lax.fori_loop(0, 4 * n_q, one, 0)

    def general_stretch(hi, slot):
        def one(qi, c):
            mask = key_minus_token() <= (query_block(qi) - k_ctx[slot]) * PAGE
            general_add(qi, ks[hi, STRETCH_AT : STRETCH_AT + PAGE], ks[hi, STRETCH_AT + PAGE : FIRST_ROWS], mask)
            return c

        lax.fori_loop(0, n_q, one, 0)

    if not has_prior:
        state[...] = jnp.zeros((n_q, STATE_ROWS, ROWS), jnp.float32)

    @pl.when(safe)
    def _():
        def add_entry(t):
            qi, hi = table[t] // n_h, table[t] % n_h
            fast_add(qi, raw_scores(qi, ks[hi, :HALF]), values_of(hi))

        def step(t, c):
            add_entry(2 * t)
            add_entry(2 * t + 1)
            return c

        lax.fori_loop(0, count // 2, step, 0)

        @pl.when(count % 2 == 1)
        def _():
            add_entry(count - 1)

        lax.fori_loop(0, jnp.where(edge_valid > 0, n_q, 0), fold_edge, 0)
        if with_stretch:
            lax.fori_loop(0, stretches, fold_stretch, 0)

    @pl.when(jnp.logical_not(safe))
    def _():
        for i in range(n_q):
            state[i, 136:] = jnp.broadcast_to(effective(state[i])[1], (8, ROWS))
        for hi, (_, _, slot, half) in enumerate(parts):
            general_part(hi, slot, half)
        for hi, slot in with_stretch:
            general_stretch(hi, slot)

    for i in range(n_q):
        if not message:
            outs[i][...] = state[i]
            continue
        total, top = effective(state[i])
        sent = jnp.where(top > EMPTY, 4.0 * jnp.ceil(top * 0.25), EMPTY)
        factor = jnp.exp2(top - sent)
        total = total * factor
        high = total.astype(jnp.bfloat16).astype(jnp.float32)
        row = lax.broadcasted_iota(jnp.int32, (16, ROWS), 0)
        tail = jnp.where(row == 0, high, jnp.where(row == 1, total - high, jnp.where(row == 2, sent, 0.0)))
        outs[i][:128] = (state[i, :128] * factor).astype(jnp.bfloat16)
        outs[i][128:] = tail.astype(jnp.bfloat16)


def whole_block(array, slot):
    return [(array, 0, slot, 0), (array, FIRST_ROWS, slot, 1)]


def fold(start, queries, q_at, halves, prior=(), message=False, cost=1.0, name="fold"):
    arrays = []
    for array, *_ in halves:
        if not any(array is other for other in arrays):
            arrays.append(array)
    parts = tuple(
        (next(i for i, other in enumerate(arrays) if other is array), row, slot, half)
        for array, row, slot, half in halves
    )
    n_q, n_h = len(queries), len(parts)
    anywhere = pl.BlockSpec(memory_space=pl.ANY)
    inputs = list(queries) + arrays + list(prior)
    work = 4 * n_q * n_h * ROWS * HALF * HEAD
    return pl.pallas_call(
        functools.partial(
            fold_kernel, n_q=n_q, q_at=q_at, n_in=len(arrays), parts=parts, has_prior=bool(prior), message=message
        ),
        out_shape=[jax.ShapeDtypeStruct((STATE_ROWS, ROWS), jnp.bfloat16 if message else jnp.float32)] * n_q,
        in_specs=[pl.BlockSpec(memory_space=pltpu.SMEM)] + [anywhere] * len(inputs),
        scratch_shapes=[
            pltpu.VMEM((n_q, QUERY_ROWS, HEAD), jnp.bfloat16),
            pltpu.VMEM((n_h, FIRST_ROWS, HEAD), jnp.bfloat16),
            pltpu.VMEM((n_q, STATE_ROWS, ROWS), jnp.float32),
            pltpu.SMEM((n_q * n_h + 1,), jnp.int32),
            pltpu.SMEM((n_q * n_h + 1,), jnp.int32),
            pltpu.SemaphoreType.DMA((len(inputs) + n_h,)),
        ],
        compiler_params=pltpu.CompilerParams(vmem_limit_bytes=48 << 20),
        cost_estimate=pl.CostEstimate(
            flops=int(2 * work * cost), transcendentals=0, bytes_accessed=int(n_h * 300000 * cost)
        ),
        name=name,
    )(start, *inputs)


def merge_kernel(own_ref, *refs):
    message_refs, out_ref = refs[:-1], refs[-1]
    total, top = effective(own_ref)
    tops, totals, sums = [top], [total], [own_ref[:128]]
    for ref in message_refs:
        tail = ref[128:].astype(jnp.float32)
        tops.append(tail[2:3])
        totals.append(tail[0:1] + tail[1:2])
        sums.append(ref[:128].astype(jnp.float32))
    top = functools.reduce(jnp.maximum, tops)
    factors = [jnp.exp2(t - top) for t in tops]
    total = functools.reduce(jnp.add, [t * f for t, f in zip(totals, factors)])
    inverse = 1.0 / total
    attended = functools.reduce(jnp.add, [s * (f * inverse) for s, f in zip(sums, factors)])
    for h in range(GROUP):
        columns = slice(h * HEAD, (h + 1) * HEAD)
        out_ref[0, :, columns] = attended[:, columns].T.astype(jnp.bfloat16)


def merge(own, messages):
    return pl.pallas_call(
        merge_kernel,
        out_shape=jax.ShapeDtypeStruct((1, PAGE, ROWS), jnp.bfloat16),
        compiler_params=pltpu.CompilerParams(vmem_limit_bytes=16 << 20),
        name="merge",
    )(own, *messages)


def received(page_rows, row_count):
    block = lax.axis_index("group") * 16 + lax.axis_index("ctx")
    kind = block % 4
    far = jnp.where(kind % 2 == 0, page_rows[(block + 16) % 32] - block * row_count, -1)
    source = jnp.where(kind == 3, block - block % 16 + (block + 8) % 16, jnp.maximum(block - 1, 0))
    near = jnp.where(kind >= 2, page_rows[source] - block * row_count, -1)
    return far, near


def scores_for(queries, keys):
    return lax.dot_general(queries, keys, (((1,), (1,)), ((), ())), preferred_element_type=jnp.float32) * SCALE2


def decode_kernel(page_rows, lengths, q_ref, cache_ref, draft_ref, out_ref, sum_ref, stat_ref, *, row_count):
    block_rows, rows, _ = q_ref.shape
    steps, limit = draft_ref.shape[2], cache_ref.shape[2]
    far, near = received(page_rows, row_count)
    for i in range(block_rows):
        r = pl.program_id(0) * block_rows + i
        length = lengths[r]
        first = jnp.where((r == far) | (r == near), PAGE, 0)
        queries = q_ref[i]
        position = lax.broadcasted_iota(jnp.int32, (rows, limit), 1)
        scores = scores_for(queries, cache_ref[0, i])
        scores = jnp.where((position >= first) & (position < length), scores, -jnp.inf)
        draft = scores_for(queries, draft_ref[0, i])
        step = lax.broadcasted_iota(jnp.int32, (rows, steps), 0) // GROUP
        draft = jnp.where(lax.broadcasted_iota(jnp.int32, (rows, steps), 1) <= step, draft, -jnp.inf)
        top = jnp.maximum(jnp.max(scores, axis=1, keepdims=True), jnp.max(draft, axis=1, keepdims=True))
        weights, draft_weights = jnp.exp2(scores - top), jnp.exp2(draft - top)
        total = jnp.sum(weights, axis=1, keepdims=True) + jnp.sum(draft_weights, axis=1, keepdims=True)
        summed = jnp.dot(weights.astype(jnp.bfloat16), cache_ref[1, i], preferred_element_type=jnp.float32)
        summed += jnp.dot(draft_weights.astype(jnp.bfloat16), draft_ref[1, i], preferred_element_type=jnp.float32)
        out_ref[i] = (summed / total).astype(jnp.bfloat16)
        sum_ref[i] = summed
        lane = lax.broadcasted_iota(jnp.int32, (rows, HEAD), 1)
        stat_ref[i] = jnp.where(lane == 0, total, top)


def decode(page_rows, lengths, queries, cache, draft):
    row_count, rows, _ = queries.shape
    steps, limit = draft.shape[2], cache.shape[2]
    block_rows = 4
    smem = pl.BlockSpec(memory_space=pltpu.SMEM)
    row_spec = pl.BlockSpec((block_rows, rows, HEAD), lambda r: (r, 0, 0))
    return pl.pallas_call(
        functools.partial(decode_kernel, row_count=row_count),
        grid=(row_count // block_rows,),
        out_shape=[jax.ShapeDtypeStruct(queries.shape, t) for t in (jnp.bfloat16, jnp.float32, jnp.float32)],
        in_specs=[
            smem,
            smem,
            row_spec,
            pl.BlockSpec((2, block_rows, limit, HEAD), lambda r: (0, r, 0, 0)),
            pl.BlockSpec((2, block_rows, steps, HEAD), lambda r: (0, r, 0, 0)),
        ],
        out_specs=[row_spec] * 3,
        compiler_params=pltpu.CompilerParams(vmem_limit_bytes=24 << 20),
        cost_estimate=pl.CostEstimate(flops=8 * row_count * rows * limit * HEAD, transcendentals=0, bytes_accessed=16 << 20),
        name="decode",
    )(page_rows, lengths, queries, pltpu.with_memory_space_constraint(cache, pltpu.HBM), draft)


def page_kernel(page_rows, q_ref, out_in, sum_ref, stat_ref, far_page, near_page, out_ref):
    row_count, rows, _ = q_ref.shape
    out_ref[...] = out_in[...]
    for r, page in zip(received(page_rows, row_count), (far_page, near_page)):

        @pl.when(r >= 0)
        def _():
            scores = scores_for(q_ref[r], page[0])
            before = stat_ref[r, :, 1:2]
            top = jnp.maximum(before, jnp.max(scores, axis=1, keepdims=True))
            factor = jnp.exp2(before - top)
            weights = jnp.exp2(scores - top)
            total = stat_ref[r, :, 0:1] * factor + jnp.sum(weights, axis=1, keepdims=True)
            summed = jnp.dot(weights.astype(jnp.bfloat16), page[1], preferred_element_type=jnp.float32)
            out_ref[r] = ((sum_ref[r] * factor + summed) / total).astype(jnp.bfloat16)


def with_pages(page_rows, queries, decoded, far_page, near_page):
    return pl.pallas_call(
        page_kernel,
        out_shape=jax.ShapeDtypeStruct(queries.shape, jnp.bfloat16),
        in_specs=[pl.BlockSpec(memory_space=pltpu.SMEM)] + [pl.BlockSpec(memory_space=pltpu.VMEM)] * 6,
        compiler_params=pltpu.CompilerParams(vmem_limit_bytes=16 << 20),
        name="pages",
    )(page_rows, queries, *decoded, far_page, near_page)


def near_pages():
    return [(c, c + 1) for c in range(1, 16, 4)] + [(c, (c + 8) % 16) for c in range(3, 16, 4)]


def on_device(
    stretch_query,
    prefix_keyvals,
    stretch_key_values,
    stretch_start,
    decode_query,
    draft_key_values,
    decode_cache,
    cache_lengths,
    page_rows,
):
    row_count, steps, _ = decode_query.shape
    send = lambda x, dz, dy: lax.ppermute(x, "ctx", xor_pairs(dz, dy))
    after = lambda x, *results: lax.optimization_barrier((x, *results))[0]
    query, own, own_first, own_second = prepare(stretch_query, prefix_keyvals, stretch_key_values)
    z_first = send(own_first, 2, 0)
    keys_y = send(own, 0, 1)
    query_y = send(query, 0, 3)
    query_z = send(query, 1, 0)
    query_d = send(query, 1, 3)
    z_second = send(own_second, 2, 0)
    d_first = send(z_first, 0, 1)

    decode_rows = decode_query.reshape(row_count, steps * GROUP, HEAD)
    decoded = decode(page_rows, cache_lengths, decode_rows, decode_cache, draft_key_values)
    start = after(stretch_start, *decoded)
    near_source = after(stretch_key_values[0], *decoded)
    near_page = lax.ppermute(near_source, "ctx", near_pages())
    far_page = lax.ppermute(near_source, ("group", "ctx"), [(n, (n + 16) % 32) for n in range(0, 32, 2)])

    others = [query_d, query_z, query_y]
    own_block, y_block = whole_block(own, 0), whole_block(keys_y, 1)
    z_block = [(z_first, 0, 2, 0), (z_second, 0, 2, 1)]
    states = fold(start, others, 1, own_block + y_block + z_block[:1], name="fold_first")
    z_second_late = after(z_second, *states)
    d_second = send(z_second_late, 0, 1)
    d_block = [(d_first, 0, 3, 0), (d_second, 0, 3, 1)]
    states = fold(
        start, others, 1, [(z_second_late, 0, 2, 1), d_block[0]], prior=states, name="fold_second"
    )
    messages = fold(start, others, 1, d_block[1:], prior=states, message=True, name="fold_third")
    from_d = send(messages[0], 1, 3)
    from_z = send(messages[1], 1, 0)
    from_y = send(messages[2], 0, 3)
    start = after(start, *messages)
    (final,) = fold(start, [query], 0, own_block + y_block + z_block + d_block, name="fold_own")
    decode_rows = after(decode_rows, final)
    decode_out = with_pages(page_rows, decode_rows, decoded, far_page, near_page).reshape(decode_query.shape)
    final = after(final, decode_out)
    prefill_out = merge(final, [from_y, from_z, from_d])
    return (prefill_out, decode_out)


def solution(mesh):
    return jax.shard_map(
        on_device,
        mesh=mesh,
        in_specs=(
            P("group", "ctx", "tp"),
            P("group", None, "ctx", "tp"),
            P("group", None, "ctx", "tp"),
            P("group"),
            P(("group", "ctx"), None, "tp"),
            P(None, ("group", "ctx"), None, "tp"),
            P(None, ("group", "ctx"), None, "tp"),
            P(("group", "ctx")),
            P(),
        ),
        out_specs=(P("group", "ctx", "tp"), P(("group", "ctx"), None, "tp")),
        check_vma=False,
    )
```

time: 356 us -> 125 us (0.35)
  matrix products: 139 us -> 0 us
  waiting for transfers between devices: 103 us -> 1.27 us
  Pallas kernels: 0 us -> 91.1 us
  other arithmetic: 43.6 us -> 0 us
  blocking collectives: 35.1 us -> 0 us
  starting transfers between devices: 5.93 us -> 26.8 us
  between operations: 14.2 us -> 1.45 us
  local copies, waits for them, and re-layouts: 8.86 us -> 3.72 us
    dot_general x91 -> x0, matrix products: 139 us -> none  [the longest x36 67 us: absorb_step(): jnp.einsum('kgts,skd->kgtd', weights, value_block, preferred_element_type...]
    pallas_call x0 -> x8, Pallas kernels: none -> 91.1 us  [the longest x4 79.4 us: fold(): pl.pallas_call(functools.partial(fold_kernel, n_q=n_q, q_at=q_at, n_in=le...]
    all_gather x1 -> x0, waiting for transfers between devices: 67.1 us -> none  [on_device(): lax.all_gather(prefix_keyvals, 'ctx', axis=2, tiled=True)]
    all_to_all x1 -> x0, waiting for transfers between devices: 35.2 us -> none  [copy_for_each(): return lax.all_to_all(copies, axis, split_axis=0, concat_axis=0, tiled=True)]
    all_to_all x1 -> x0, blocking collectives: 35.1 us -> none  [copy_for_each(): return lax.all_to_all(copies, axis, split_axis=0, concat_axis=0, tiled=True)]
    ppermute x0 -> x13, starting transfers between devices: none -> 26.8 us  [the longest x11 18 us: on_device(): send = lambda x, dz, dy: lax.ppermute(x, 'ctx', xor_pairs(dz, dy))]
    lt x40 -> x0, other arithmetic: 21.5 us -> none  [the longest x32 20.9 us: absorb_step(): allowed = (key_pos < limit)[None, :]]
    reduce_sum x45 -> x0, other arithmetic: 19.4 us -> none  [refresh(): totals = totals * factor + jnp.sum(weights, axis=-1)]
  transfers between devices with their start and end apart: 2 -> 13, of which waited for: 2 -> 1; matrix products, arithmetic and copies ran while one was open for 9% -> 1% of each run, Pallas kernels for 0% -> 71%
where the time goes in v2:
time: 125 us; the launch traced here: 124 us
  Pallas kernels  91.1 us (73%)
  starting transfers between devices  26.8 us (21%)
  local copies, waits for them, and re-layouts  3.72 us (3%)
  between operations  1.45 us (1%)
  waiting for transfers between devices  1.27 us (1%)
    pallas_call x4, Pallas kernels, fold(): pl.pallas_call(functools.partial(fold_kernel, n_q=n_q, q_at=q_at, n_in=le...  79.4 us
    ppermute x11, starting transfers between devices, on_device(): send = lambda x, dz, dy: lax.ppermute(x, 'ctx', xor_pairs(dz, dy))  18 us
    ppermute x1, starting transfers between devices, on_device(): lax.ppermute(near_source, ('group', 'ctx'), [(n, (n + 16) % 32) for n in...  8.21 us
    pallas_call x1, Pallas kernels, decode(): pl.pallas_call(functools.partial(decode_kernel, row_count=row_count), gri...  7.46 us
  transfers between devices with their start and end apart: 13, of which 1 were waited for; matrix products, arithmetic and copies ran while one was open for 1% of the time, Pallas kernels for 71%

profile of v2, /device:TPU:2, one launch (start us, length us, event | category | flops | bytes accessed | tf_op | source)
XLA Modules:
  0.0 124.3 jit_solution(18019079045957551455)
XLA Ops:
  0.6 2.2 %prepare.1 = (bf16[1040,128]{1,0:T(8,128)(2,1)S(1)}, bf16[2336,128]{1,0:T(8,128)(2,1)S(1)}, bf16[1296,128]{1,0:T(8,128)(2,1)S(1)}, bf16[1040,128]{1,0:T(8,128)(2,1)S(1)}) custom-call(bf16[1,128,1024]{2,1,0:T(8,128)(2,1)} %query_hbm.1, bf16[1,2,1024,128]{3,2,1,0:T(8,128)(2,1)} %prefix_hbm.1, bf16[1,2,128,128]{3,2,1,0:T(8,128)(2,1)} %stretch_hbm.1), custom_call_target="tpu_custom_call" | custom-call | tf_op jit(solution)/shard_map/prepare/pallas_call | solution.py:81
  2.8 1.7 %collective-permute-start.4 = (bf16[2336,128]{1,0:T(8,128)(2,1)S(1)}, bf16[2336,128]{1,0:T(8,128)(2,1)S(1)}, u32[]{:S(2)}, u32[]{:S(2)}) collective-permute-start(bf16[2336,128]{1,0:T(8,128)(2,1)S(1)} %get-tuple-element.30.refs_3_.refs_1_), channel_id=1, source_target_pairs={{0,8},{8,0},{16,24},{24,16},{32,40},{40,32},{48,56},{56,48},{64,72... | collective-permute-start | bytes 1794056 | tf_op jit(solution)/shard_map/ppermute | solution.py:436
  4.5 3.3 %collective-permute-start.5 = (bf16[1296,128]{1,0:T(8,128)(2,1)S(1)}, bf16[1296,128]{1,0:T(8,128)(2,1)S(1)}, u32[]{:S(2)}, u32[]{:S(2)}) collective-permute-start(bf16[1296,128]{1,0:T(8,128)(2,1)S(1)} %get-tuple-element.31), channel_id=1, source_target_pairs={{0,64},{8,72},{16,80},{24,88},{32,96},{40,104},{48,112},{56,120},{... | collective-permute-start | bytes 995336 | tf_op jit(solution)/shard_map/ppermute | solution.py:436
  7.7 3.5 %collective-permute-start = (bf16[1040,128]{1,0:T(8,128)(2,1)S(1)}, bf16[1040,128]{1,0:T(8,128)(2,1)S(1)}, u32[]{:S(2)}, u32[]{:S(2)}) collective-permute-start(bf16[1040,128]{1,0:T(8,128)(2,1)S(1)} %get-tuple-element.28.refs_0_), channel_id=1, source_target_pairs={{0,56},{8,48},{16,40},{24,32},{32,24},{40,16},{48,8},{56,0},{64,12... | collective-permute-start | bytes 798728 | tf_op jit(solution)/shard_map/ppermute | solution.py:436
  11.3 0.1 collective-permute-start.1
  11.4 1.1 collective-permute-start.2
  13.1 1.0 reshape.10.q_ref
  14.0 0.0 copy-start
  14.1 0.7 copy-done
  14.8 0.7 copy-done.1
  15.5 0.7 copy-done.3
  16.1 7.5 %decode.1 = (bf16[16,32,128]{2,1,0:T(8,128)(2,1)S(1)}, f32[16,32,128]{2,1,0:T(8,128)S(1)}, f32[16,32,128]{2,1,0:T(8,128)S(1)}) custom-call(s32[32]{0:T(128)S(1)} %copy-done.1, s32[16]{0:T(128)S(1)} %copy-done.3, bf16[16,32,128]{2,1,0:T(8,128)(2,1)S(1)} %reshape.10.q_ref, bf16[2,16,1024,128]{3,2,1,0:T(8,128)(2,1)} %cache_ref.1, ...), custom_call_target="tpu_custom_call" | custom-call | flops 536870912 | bytes 16777216 | tf_op jit(solution)/shard_map/decode/pallas_call | solution.py:375
  23.6 1.2 collective-permute-done.refs_0_
  24.8 8.2 %collective-permute-start.8 = (bf16[2,128,128]{2,1,0:T(8,128)(2,1)}, bf16[2,128,128]{2,1,0:T(8,128)(2,1)S(1)}, u32[]{:S(2)}, u32[]{:S(2)}) collective-permute-start(bf16[2,128,128]{2,1,0:T(8,128)(2,1)} %bitcast), channel_id=1, source_target_pairs={{0,128},{16,144},{32,160},{48,176},{64,192},{80,208},{96,224},{112... | collective-permute-start | bytes 196616 | tf_op jit(solution)/shard_map/ppermute | solution.py:452
  33.1 0.0 collective-permute-done.1.refs_1_
  33.1 0.7 collective-permute-start.9
  33.7 0.0 collective-permute-done.2.refs_2_
  33.8 0.6 collective-permute-start.3
  34.3 0.0 collective-permute-done.5.refs_5_.refs_3_
  34.3 2.5 %collective-permute-start.7 = (bf16[1296,128]{1,0:T(8,128)(2,1)S(1)}, bf16[1296,128]{1,0:T(8,128)(2,1)S(1)}, u32[]{:S(2)}, u32[]{:S(2)}) collective-permute-start(bf16[1296,128]{1,0:T(8,128)(2,1)S(1)} %collective-permute-done.5.refs_5_.refs_3_), channel_id=1, source_target_pairs={{0,8},{8,0},{16,24},{24,16},{32,40},{40,32},{48,56},{56,48},{64,72... | collective-permute-start | bytes 995336 | tf_op jit(solution)/shard_map/ppermute | solution.py:436
  36.9 36.8 %fold_first.1 = (f32[144,1024]{1,0:T(8,128)S(1)}, f32[144,1024]{1,0:T(8,128)S(1)}, f32[144,1024]{1,0:T(8,128)S(1)}) custom-call(s32[1]{0:T(128)S(6)} %copy.11.start, bf16[1040,128]{1,0:T(8,128)(2,1)S(1)} %collective-permute-done.refs_0_, bf16[1040,128]{1,0:T(8,128)(2,1)S(1)} %collective-permute-done.1.refs_1_, ...), custom_call_target="tpu_custom_call" | custom-call | flops 8053063680 | bytes 1500000 | tf_op jit(solution)/shard_map/fold_first/pallas_call | solution.py:280
  73.7 0.1 collective-permute-start.6
  73.8 15.3 %fold_second.1 = (f32[144,1024]{1,0:T(8,128)S(1)}, f32[144,1024]{1,0:T(8,128)S(1)}, f32[144,1024]{1,0:T(8,128)S(1)}) custom-call(s32[1]{0:T(128)S(6)} %copy.11.start, bf16[1040,128]{1,0:T(8,128)(2,1)S(1)} %collective-permute-done.refs_0_, bf16[1040,128]{1,0:T(8,128)(2,1)S(1)} %collective-permute-done.1.refs_1_, ...), custom_call_target="tpu_custom_call" | custom-call | flops 3221225472 | bytes 600000 | tf_op jit(solution)/shard_map/fold_second/pallas_call | solution.py:280
  89.1 7.9 %fold_third.1 = (bf16[144,1024]{1,0:T(8,128)(2,1)}, bf16[144,1024]{1,0:T(8,128)(2,1)}, bf16[144,1024]{1,0:T(8,128)(2,1)}) custom-call(s32[1]{0:T(128)S(6)} %copy.11.start, bf16[1040,128]{1,0:T(8,128)(2,1)S(1)} %collective-permute-done.refs_0_, bf16[1040,128]{1,0:T(8,128)(2,1)S(1)} %collective-permute-done.1.refs_1_, ...), custom_call_target="tpu_custom_call" | custom-call | flops 1610612736 | bytes 300000 | tf_op jit(solution)/shard_map/fold_third/pallas_call | solution.py:280
  97.1 0.0 copy-start.2
  97.1 0.1 collective-permute-start.10
  97.2 2.4 %collective-permute-start.11 = (bf16[144,1024]{1,0:T(8,128)(2,1)}, bf16[144,1024]{1,0:T(8,128)(2,1)S(1)}, u32[]{:S(2)}, u32[]{:S(2)}) collective-permute-start(bf16[144,1024]{1,0:T(8,128)(2,1)} %get-tuple-element.40), channel_id=1, source_target_pairs={{0,32},{8,40},{16,48},{24,56},{32,0},{40,8},{48,16},{56,24},{64,96... | collective-permute-start | bytes 884744 | tf_op jit(solution)/shard_map/ppermute | solution.py:436
  99.6 2.6 %collective-permute-start.12 = (bf16[144,1024]{1,0:T(8,128)(2,1)}, bf16[144,1024]{1,0:T(8,128)(2,1)S(1)}, u32[]{:S(2)}, u32[]{:S(2)}) collective-permute-start(bf16[144,1024]{1,0:T(8,128)(2,1)} %get-tuple-element.39), channel_id=1, source_target_pairs={{0,56},{8,48},{16,40},{24,32},{32,24},{40,16},{48,8},{56,0},{64,12... | collective-permute-start | bytes 884744 | tf_op jit(solution)/shard_map/ppermute | solution.py:436
  102.2 19.3 %fold_own.1.own_ref = f32[144,1024]{1,0:T(8,128)S(1)} custom-call(s32[1]{0:T(128)S(6)} %copy.11.start, bf16[1040,128]{1,0:T(8,128)(2,1)S(1)} %get-tuple-element.28.refs_0_, bf16[2336,128]{1,0:T(8,128)(2,1)S(1)} %get-tuple-element.30.refs_3_.refs_1_, bf16[2336,128]{1,0:T(8,128)(2,1)S(1)} %collective-permute-done.4.refs_4_.refs_2_, ...), custom_call_target="tpu_custom_call" | custom-call | flops 4294967296 | bytes 2400000 | tf_op jit(solution)/shard_map/fold_own/pallas_call | solution.py:280
  121.6 1.0 pages.1
  122.6 0.7 reshape.11
  123.3 1.0 merge.1
  (12 shorter events, 0.0 us)
Async XLA Ops:
  2.8 34.1 %collective-permute-start.4 = (bf16[2336,128]{1,0:T(8,128)(2,1)S(1)}, bf16[2336,128]{1,0:T(8,128)(2,1)S(1)}, u32[]{:S(2)}, u32[]{:S(2)}) collective-permute-start(bf16[2336,128]{1,0:T(8,128)(2,1)S(1)} %get-tuple-element.30.refs_3_.refs_1_), channel_id=1, source_target_pairs={{0,8},{8,0},{16,24},{24,16},{32,40},{40,32},{48,56},{56,48},{64,72... | collective-permute-start | bytes 1794056 | tf_op jit(solution)/shard_map/ppermute | solution.py:436
  4.5 29.9 %collective-permute-start.5 = (bf16[1296,128]{1,0:T(8,128)(2,1)S(1)}, bf16[1296,128]{1,0:T(8,128)(2,1)S(1)}, u32[]{:S(2)}, u32[]{:S(2)}) collective-permute-start(bf16[1296,128]{1,0:T(8,128)(2,1)S(1)} %get-tuple-element.31), channel_id=1, source_target_pairs={{0,64},{8,72},{16,80},{24,88},{32,96},{40,104},{48,112},{56,120},{... | collective-permute-start | bytes 995336 | tf_op jit(solution)/shard_map/ppermute | solution.py:436
  7.7 17.1 %collective-permute-start = (bf16[1040,128]{1,0:T(8,128)(2,1)S(1)}, bf16[1040,128]{1,0:T(8,128)(2,1)S(1)}, u32[]{:S(2)}, u32[]{:S(2)}) collective-permute-start(bf16[1040,128]{1,0:T(8,128)(2,1)S(1)} %get-tuple-element.28.refs_0_), channel_id=1, source_target_pairs={{0,56},{8,48},{16,40},{24,32},{32,24},{40,16},{48,8},{56,0},{64,12... | collective-permute-start | bytes 798728 | tf_op jit(solution)/shard_map/ppermute | solution.py:436
  11.3 21.8 %collective-permute-start.1 = (bf16[1040,128]{1,0:T(8,128)(2,1)S(1)}, bf16[1040,128]{1,0:T(8,128)(2,1)S(1)}, u32[]{:S(2)}, u32[]{:S(2)}) collective-permute-start(bf16[1040,128]{1,0:T(8,128)(2,1)S(1)} %get-tuple-element.28.refs_0_), channel_id=1, source_target_pairs={{0,32},{8,40},{16,48},{24,56},{32,0},{40,8},{48,16},{56,24},{64,96... | collective-permute-start | bytes 798728 | tf_op jit(solution)/shard_map/ppermute | solution.py:436
  11.4 22.4 %collective-permute-start.2 = (bf16[1040,128]{1,0:T(8,128)(2,1)S(1)}, bf16[1040,128]{1,0:T(8,128)(2,1)S(1)}, u32[]{:S(2)}, u32[]{:S(2)}) collective-permute-start(bf16[1040,128]{1,0:T(8,128)(2,1)S(1)} %get-tuple-element.28.refs_0_), channel_id=1, source_target_pairs={{0,24},{8,16},{16,8},{24,0},{32,56},{40,48},{48,40},{56,32},{64,88... | collective-permute-start | bytes 798728 | tf_op jit(solution)/shard_map/ppermute | solution.py:436
  14.0 0.8 copy-start
  14.8 0.7 copy-start.1
  15.5 0.7 copy-start.3
  24.8 96.7 %collective-permute-start.8 = (bf16[2,128,128]{2,1,0:T(8,128)(2,1)}, bf16[2,128,128]{2,1,0:T(8,128)(2,1)S(1)}, u32[]{:S(2)}, u32[]{:S(2)}) collective-permute-start(bf16[2,128,128]{2,1,0:T(8,128)(2,1)} %bitcast), channel_id=1, source_target_pairs={{0,128},{16,144},{32,160},{48,176},{64,192},{80,208},{96,224},{112... | collective-permute-start | bytes 196616 | tf_op jit(solution)/shard_map/ppermute | solution.py:452
  33.1 88.5 %collective-permute-start.9 = (bf16[2,128,128]{2,1,0:T(8,128)(2,1)}, bf16[2,128,128]{2,1,0:T(8,128)(2,1)S(1)}, u32[]{:S(2)}, u32[]{:S(2)}) collective-permute-start(bf16[2,128,128]{2,1,0:T(8,128)(2,1)} %bitcast), channel_id=1, source_target_pairs={{8,16},{40,48},{72,80},{104,112},{24,88},{56,120},{88,24},{120,56}... | collective-permute-start | bytes 196616 | tf_op jit(solution)/shard_map/ppermute | solution.py:451
  33.8 40.0 %collective-permute-start.3 = (bf16[1040,128]{1,0:T(8,128)(2,1)S(1)}, bf16[1040,128]{1,0:T(8,128)(2,1)S(1)}, u32[]{:S(2)}, u32[]{:S(2)}) collective-permute-start(bf16[1040,128]{1,0:T(8,128)(2,1)S(1)} %get-tuple-element.29), channel_id=1, source_target_pairs={{0,64},{8,72},{16,80},{24,88},{32,96},{40,104},{48,112},{56,120},{... | collective-permute-start | bytes 798728 | tf_op jit(solution)/shard_map/ppermute | solution.py:436
  34.3 39.5 %collective-permute-start.7 = (bf16[1296,128]{1,0:T(8,128)(2,1)S(1)}, bf16[1296,128]{1,0:T(8,128)(2,1)S(1)}, u32[]{:S(2)}, u32[]{:S(2)}) collective-permute-start(bf16[1296,128]{1,0:T(8,128)(2,1)S(1)} %collective-permute-done.5.refs_5_.refs_3_), channel_id=1, source_target_pairs={{0,8},{8,0},{16,24},{24,16},{32,40},{40,32},{48,56},{56,48},{64,72... | collective-permute-start | bytes 995336 | tf_op jit(solution)/shard_map/ppermute | solution.py:436
  73.7 15.4 %collective-permute-start.6 = (bf16[1040,128]{1,0:T(8,128)(2,1)S(1)}, bf16[1040,128]{1,0:T(8,128)(2,1)S(1)}, u32[]{:S(2)}, u32[]{:S(2)}) collective-permute-start(bf16[1040,128]{1,0:T(8,128)(2,1)S(1)} %collective-permute-done.3.refs_3_.refs_4_), channel_id=1, source_target_pairs={{0,8},{8,0},{16,24},{24,16},{32,40},{40,32},{48,56},{56,48},{64,72... | collective-permute-start | bytes 798728 | tf_op jit(solution)/shard_map/ppermute | solution.py:436
  97.1 24.5 %copy-start.2 = (s32[32]{0:T(128)S(1)}, s32[32]{0:T(128)}, u32[]{:S(2)}) copy-start(s32[32]{0:T(128)} %page_rows.3) | copy-start | bytes 388
  97.1 26.2 %collective-permute-start.10 = (bf16[144,1024]{1,0:T(8,128)(2,1)}, bf16[144,1024]{1,0:T(8,128)(2,1)S(1)}, u32[]{:S(2)}, u32[]{:S(2)}) collective-permute-start(bf16[144,1024]{1,0:T(8,128)(2,1)} %get-tuple-element.41), channel_id=1, source_target_pairs={{0,24},{8,16},{16,8},{24,0},{32,56},{40,48},{48,40},{56,32},{64,88... | collective-permute-start | bytes 884744 | tf_op jit(solution)/shard_map/ppermute | solution.py:436
  97.2 26.1 %collective-permute-start.11 = (bf16[144,1024]{1,0:T(8,128)(2,1)}, bf16[144,1024]{1,0:T(8,128)(2,1)S(1)}, u32[]{:S(2)}, u32[]{:S(2)}) collective-permute-start(bf16[144,1024]{1,0:T(8,128)(2,1)} %get-tuple-element.40), channel_id=1, source_target_pairs={{0,32},{8,40},{16,48},{24,56},{32,0},{40,8},{48,16},{56,24},{64,96... | collective-permute-start | bytes 884744 | tf_op jit(solution)/shard_map/ppermute | solution.py:436
  99.6 23.7 %collective-permute-start.12 = (bf16[144,1024]{1,0:T(8,128)(2,1)}, bf16[144,1024]{1,0:T(8,128)(2,1)S(1)}, u32[]{:S(2)}, u32[]{:S(2)}) collective-permute-start(bf16[144,1024]{1,0:T(8,128)(2,1)} %get-tuple-element.39), channel_id=1, source_target_pairs={{0,56},{8,48},{16,40},{24,32},{32,24},{40,16},{48,8},{56,0},{64,12... | collective-permute-start | bytes 884744 | tf_op jit(solution)/shard_map/ppermute | solution.py:436

commit v3 on v2

--- a/solution.py
+++ b/solution.py
@@ -63,14 +63,15 @@
     for made in copies[GROUP:]:
         made.wait()
     norms = norm_rows(keys[...])
-    for at, part, base in ((0, first, 0), (HALF, second, FIRST_ROWS)):
-        pieces = [(0, keys[at : at + HALF]), (NORM_AT, norms)]
-        pieces += [(HALF + j, values[at + j : at + j + PAGE].T) for j in range(0, HALF, PAGE)]
-        if base == 0:
-            pieces += [(STRETCH_AT, keys[PREFIX:]), (STRETCH_AT + PAGE, values[PREFIX:].T)]
-        for row, piece in pieces:
-            part[row : row + piece.shape[0]] = piece
-            whole[base + row : base + row + piece.shape[0]] = piece
+    for at, base in ((0, 0), (HALF, FIRST_ROWS)):
+        whole[base : base + HALF] = keys[at : at + HALF]
+        for j in range(0, HALF, PAGE):
+            whole[base + HALF + j : base + HALF + j + PAGE] = values[at + j : at + j + PAGE].T
+        whole[base + NORM_AT : base + STRETCH_AT] = norms
+    whole[STRETCH_AT : STRETCH_AT + PAGE] = keys[PREFIX:]
+    whole[STRETCH_AT + PAGE : FIRST_ROWS] = values[PREFIX:].T
+    first[...] = whole[:FIRST_ROWS]
+    second[...] = whole[FIRST_ROWS:]
     for made in copies[:GROUP]:
         made.wait()
     query_msg[ROWS:] = norm_rows(query_msg[:ROWS])
@@ -344,32 +345,35 @@
     block_rows, rows, _ = q_ref.shape
     steps, limit = draft_ref.shape[2], cache_ref.shape[2]
     far, near = received(page_rows, row_count)
-    for i in range(block_rows):
+    every = range(block_rows)
+    cached = [scores_for(q_ref[i], cache_ref[0, i]) for i in every]
+    drafted = [scores_for(q_ref[i], draft_ref[0, i]) for i in every]
+    position = lax.broadcasted_iota(jnp.int32, (rows, limit), 1)
+    step = lax.broadcasted_iota(jnp.int32, (rows, steps), 0) // GROUP
+    causal = lax.broadcasted_iota(jnp.int32, (rows, steps), 1) <= step
+    lane = lax.broadcasted_iota(jnp.int32, (rows, HEAD), 1)
+    pieces = []
+    for i in every:
         r = pl.program_id(0) * block_rows + i
-        length = lengths[r]
         first = jnp.where((r == far) | (r == near), PAGE, 0)
-        queries = q_ref[i]
-        position = lax.broadcasted_iota(jnp.int32, (rows, limit), 1)
-        scores = scores_for(queries, cache_ref[0, i])
-        scores = jnp.where((position >= first) & (position < length), scores, -jnp.inf)
-        draft = scores_for(queries, draft_ref[0, i])
-        step = lax.broadcasted_iota(jnp.int32, (rows, steps), 0) // GROUP
-        draft = jnp.where(lax.broadcasted_iota(jnp.int32, (rows, steps), 1) <= step, draft, -jnp.inf)
+        scores = jnp.where((position >= first) & (position < lengths[r]), cached[i], -jnp.inf)
+        draft = jnp.where(causal, drafted[i], -jnp.inf)
         top = jnp.maximum(jnp.max(scores, axis=1, keepdims=True), jnp.max(draft, axis=1, keepdims=True))
         weights, draft_weights = jnp.exp2(scores - top), jnp.exp2(draft - top)
         total = jnp.sum(weights, axis=1, keepdims=True) + jnp.sum(draft_weights, axis=1, keepdims=True)
-        summed = jnp.dot(weights.astype(jnp.bfloat16), cache_ref[1, i], preferred_element_type=jnp.float32)
-        summed += jnp.dot(draft_weights.astype(jnp.bfloat16), draft_ref[1, i], preferred_element_type=jnp.float32)
+        stat_ref[i] = jnp.where(lane == 0, total, top)
+        pieces.append((weights.astype(jnp.bfloat16), draft_weights.astype(jnp.bfloat16), total))
+    for i, (weights, draft_weights, total) in enumerate(pieces):
+        summed = jnp.dot(weights, cache_ref[1, i], preferred_element_type=jnp.float32)
+        summed += jnp.dot(draft_weights, draft_ref[1, i], preferred_element_type=jnp.float32)
         out_ref[i] = (summed / total).astype(jnp.bfloat16)
         sum_ref[i] = summed
-        lane = lax.broadcasted_iota(jnp.int32, (rows, HEAD), 1)
-        stat_ref[i] = jnp.where(lane == 0, total, top)
 
 
 def decode(page_rows, lengths, queries, cache, draft):
     row_count, rows, _ = queries.shape
     steps, limit = draft.shape[2], cache.shape[2]
-    block_rows = 4
+    block_rows = 8
     smem = pl.BlockSpec(memory_space=pltpu.SMEM)
     row_spec = pl.BlockSpec((block_rows, rows, HEAD), lambda r: (r, 0, 0))
     return pl.pallas_call(
@@ -384,10 +388,10 @@
             pl.BlockSpec((2, block_rows, steps, HEAD), lambda r: (0, r, 0, 0)),
         ],
         out_specs=[row_spec] * 3,
-        compiler_params=pltpu.CompilerParams(vmem_limit_bytes=24 << 20),
+        compiler_params=pltpu.CompilerParams(vmem_limit_bytes=32 << 20),
         cost_estimate=pl.CostEstimate(flops=8 * row_count * rows * limit * HEAD, transcendentals=0, bytes_accessed=16 << 20),
         name="decode",
-    )(page_rows, lengths, queries, pltpu.with_memory_space_constraint(cache, pltpu.HBM), draft)
+    )(page_rows, lengths, queries, *(pltpu.with_memory_space_constraint(x, pltpu.HBM) for x in (cache, draft)))
 
 
 def page_kernel(page_rows, q_ref, out_in, sum_ref, stat_ref, far_page, near_page, out_ref):
@@ -441,32 +445,27 @@
     query_y = send(query, 0, 3)
     query_z = send(query, 1, 0)
     query_d = send(query, 1, 3)
-    z_second = send(own_second, 2, 0)
     d_first = send(z_first, 0, 1)
 
     decode_rows = decode_query.reshape(row_count, steps * GROUP, HEAD)
     decoded = decode(page_rows, cache_lengths, decode_rows, decode_cache, draft_key_values)
     start = after(stretch_start, *decoded)
-    near_source = after(stretch_key_values[0], *decoded)
+    z_second = send(after(own_second, keys_y, *decoded), 2, 0)
+    d_second = send(z_second, 0, 1)
+    near_source = after(stretch_key_values[0], z_first, *decoded)
     near_page = lax.ppermute(near_source, "ctx", near_pages())
     far_page = lax.ppermute(near_source, ("group", "ctx"), [(n, (n + 16) % 32) for n in range(0, 32, 2)])
 
     others = [query_d, query_z, query_y]
-    own_block, y_block = whole_block(own, 0), whole_block(keys_y, 1)
-    z_block = [(z_first, 0, 2, 0), (z_second, 0, 2, 1)]
-    states = fold(start, others, 1, own_block + y_block + z_block[:1], name="fold_first")
-    z_second_late = after(z_second, *states)
-    d_second = send(z_second_late, 0, 1)
-    d_block = [(d_first, 0, 3, 0), (d_second, 0, 3, 1)]
-    states = fold(
-        start, others, 1, [(z_second_late, 0, 2, 1), d_block[0]], prior=states, name="fold_second"
-    )
-    messages = fold(start, others, 1, d_block[1:], prior=states, message=True, name="fold_third")
+    near = whole_block(own, 0) + whole_block(keys_y, 1) + [(z_first, 0, 2, 0), (z_second, 0, 2, 1)]
+    far = [(d_first, 0, 3, 0), (d_second, 0, 3, 1)]
+    states = fold(start, others, 1, near, name="fold_near")
+    messages = fold(start, others, 1, far, prior=states, message=True, name="fold_far")
     from_d = send(messages[0], 1, 3)
     from_z = send(messages[1], 1, 0)
     from_y = send(messages[2], 0, 3)
     start = after(start, *messages)
-    (final,) = fold(start, [query], 0, own_block + y_block + z_block + d_block, name="fold_own")
+    (final,) = fold(start, [query], 0, near + far, name="fold_own")
     decode_rows = after(decode_rows, final)
     decode_out = with_pages(page_rows, decode_rows, decoded, far_page, near_page).reshape(decode_query.shape)
     final = after(final, decode_out)

time: 125 us -> 124 us (level)
  Pallas kernels: 91.1 us -> 87.9 us
  starting transfers between devices: 26.8 us -> 29.1 us
    ppermute x11, starting transfers between devices: 18 us -> 21.1 us  [on_device(): send = lambda x, dz, dy: lax.ppermute(x, 'ctx', xor_pairs(dz, dy))]
    pallas_call x1, Pallas kernels: 7.46 us -> 5 us  [decode(): pl.pallas_call(functools.partial(decode_kernel, row_count=row_count), gri...]
    pallas_call x4 -> x3, Pallas kernels: 79.4 us -> 78.6 us  [fold(): pl.pallas_call(functools.partial(fold_kernel, n_q=n_q, q_at=q_at, n_in=le...]
  transfers between devices with their start and end apart: 13 -> 13, of which waited for: 1 -> 1; matrix products, arithmetic and copies ran while one was open for 1% -> 1% of each run, Pallas kernels for 71% -> 68%
where the time goes in v3:
time: 124 us
  Pallas kernels  87.9 us (71%)
  starting transfers between devices  29.1 us (23%)
  local copies, waits for them, and re-layouts  2.97 us (2%)
  waiting for transfers between devices  2.36 us (2%)
  between operations  1.45 us (1%)
    pallas_call x3, Pallas kernels, fold(): pl.pallas_call(functools.partial(fold_kernel, n_q=n_q, q_at=q_at, n_in=le...  78.6 us
    ppermute x11, starting transfers between devices, on_device(): send = lambda x, dz, dy: lax.ppermute(x, 'ctx', xor_pairs(dz, dy))  21.1 us
    ppermute x1, starting transfers between devices, on_device(): lax.ppermute(near_source, ('group', 'ctx'), [(n, (n + 16) % 32) for n in...  7.3 us
    pallas_call x1, Pallas kernels, decode(): pl.pallas_call(functools.partial(decode_kernel, row_count=row_count), gri...  5 us
  transfers between devices with their start and end apart: 13, of which 1 were waited for; matrix products, arithmetic and copies ran while one was open for 1% of the time, Pallas kernels for 68%

profile of v3, /device:TPU:2, one launch (start us, length us, event | category | flops | bytes accessed | tf_op | source)
XLA Modules:
  0.0 123.7 jit_solution(10253373333778036901)
XLA Ops:
  0.6 2.2 %prepare.1 = (bf16[1040,128]{1,0:T(8,128)(2,1)S(1)}, bf16[2336,128]{1,0:T(8,128)(2,1)S(1)}, bf16[1296,128]{1,0:T(8,128)(2,1)S(1)}, bf16[1040,128]{1,0:T(8,128)(2,1)S(1)}) custom-call(bf16[1,128,1024]{2,1,0:T(8,128)(2,1)} %query_hbm.1, bf16[1,2,1024,128]{3,2,1,0:T(8,128)(2,1)} %prefix_hbm.1, bf16[1,2,128,128]{3,2,1,0:T(8,128)(2,1)} %stretch_hbm.1), custom_call_target="tpu_custom_call" | custom-call | tf_op jit(solution)/shard_map/prepare/pallas_call | solution.py:82
  2.8 1.7 %collective-permute-start.5 = (bf16[2336,128]{1,0:T(8,128)(2,1)S(1)}, bf16[2336,128]{1,0:T(8,128)(2,1)S(1)}, u32[]{:S(2)}, u32[]{:S(2)}) collective-permute-start(bf16[2336,128]{1,0:T(8,128)(2,1)S(1)} %get-tuple-element.28.refs_3_.refs_1_), channel_id=1, source_target_pairs={{0,8},{8,0},{16,24},{24,16},{32,40},{40,32},{48,56},{56,48},{64,72... | collective-permute-start | bytes 1794056 | tf_op jit(solution)/shard_map/ppermute | solution.py:440
  4.5 3.3 %collective-permute-start.3 = (bf16[1296,128]{1,0:T(8,128)(2,1)S(1)}, bf16[1296,128]{1,0:T(8,128)(2,1)S(1)}, u32[]{:S(2)}, u32[]{:S(2)}) collective-permute-start(bf16[1296,128]{1,0:T(8,128)(2,1)S(1)} %get-tuple-element.26), channel_id=1, source_target_pairs={{0,64},{8,72},{16,80},{24,88},{32,96},{40,104},{48,112},{56,120},{... | collective-permute-start | bytes 995336 | tf_op jit(solution)/shard_map/ppermute | solution.py:440
  7.7 3.5 %collective-permute-start = (bf16[1040,128]{1,0:T(8,128)(2,1)S(1)}, bf16[1040,128]{1,0:T(8,128)(2,1)S(1)}, u32[]{:S(2)}, u32[]{:S(2)}) collective-permute-start(bf16[1040,128]{1,0:T(8,128)(2,1)S(1)} %get-tuple-element.25.refs_0_), channel_id=1, source_target_pairs={{0,56},{8,48},{16,40},{24,32},{32,24},{40,16},{48,8},{56,0},{64,12... | collective-permute-start | bytes 798728 | tf_op jit(solution)/shard_map/ppermute | solution.py:440
  11.3 0.1 collective-permute-start.1
  11.4 1.0 reshape.10.q_ref
  12.4 0.0 copy-start
  12.4 0.6 copy-done
  13.0 0.7 copy-done.2
  13.7 5.0 %decode.1 = (bf16[16,32,128]{2,1,0:T(8,128)(2,1)S(1)}, f32[16,32,128]{2,1,0:T(8,128)S(1)}, f32[16,32,128]{2,1,0:T(8,128)S(1)}) custom-call(s32[32]{0:T(128)S(1)} %copy-done, s32[16]{0:T(128)S(1)} %copy-done.2, bf16[16,32,128]{2,1,0:T(8,128)(2,1)S(1)} %reshape.10.q_ref, bf16[2,16,1024,128]{3,2,1,0:T(8,128)(2,1)} %cache_ref.1, bf16[2,16,4,128]{3,2,1,0:T(4,128)(2,1)} %draft_ref.1), custom_call_target="tpu_custom_call" | custom-call | flops 536870912 | bytes 16777216 | tf_op jit(solution)/shard_map/decode/pallas_call | solution.py:379
  18.7 0.0 collective-permute-done.5.refs_4_.refs_2_
  18.7 2.7 %collective-permute-start.6 = (bf16[1040,128]{1,0:T(8,128)(2,1)S(1)}, bf16[1040,128]{1,0:T(8,128)(2,1)S(1)}, u32[]{:S(2)}, u32[]{:S(2)}) collective-permute-start(bf16[1040,128]{1,0:T(8,128)(2,1)S(1)} %get-tuple-element.29), channel_id=1, source_target_pairs={{0,64},{8,72},{16,80},{24,88},{32,96},{40,104},{48,112},{56,120},{... | collective-permute-start | bytes 798728 | tf_op jit(solution)/shard_map/ppermute | solution.py:440
  21.4 3.0 %collective-permute-start.2 = (bf16[1040,128]{1,0:T(8,128)(2,1)S(1)}, bf16[1040,128]{1,0:T(8,128)(2,1)S(1)}, u32[]{:S(2)}, u32[]{:S(2)}) collective-permute-start(bf16[1040,128]{1,0:T(8,128)(2,1)S(1)} %get-tuple-element.25.refs_0_), channel_id=1, source_target_pairs={{0,24},{8,16},{16,8},{24,0},{32,56},{40,48},{48,40},{56,32},{64,88... | collective-permute-start | bytes 798728 | tf_op jit(solution)/shard_map/ppermute | solution.py:440
  25.1 7.3 %collective-permute-start.8 = (bf16[2,128,128]{2,1,0:T(8,128)(2,1)}, bf16[2,128,128]{2,1,0:T(8,128)(2,1)S(1)}, u32[]{:S(2)}, u32[]{:S(2)}) collective-permute-start(bf16[2,128,128]{2,1,0:T(8,128)(2,1)} %bitcast), channel_id=1, source_target_pairs={{0,128},{16,144},{32,160},{48,176},{64,192},{80,208},{96,224},{112... | collective-permute-start | bytes 196616 | tf_op jit(solution)/shard_map/ppermute | solution.py:457
  32.4 0.0 collective-permute-done.refs_0_
  32.4 0.7 collective-permute-start.9
  33.1 2.3 %collective-permute-done.1.refs_1_ = bf16[1040,128]{1,0:T(8,128)(2,1)S(1)} collective-permute-done((bf16[1040,128]{1,0:T(8,128)(2,1)S(1)}, bf16[1040,128]{1,0:T(8,128)(2,1)S(1)}, u32[]{:S(2)}, u32[]{:S(2)}) %collective-permute-start.1) | collective-permute-done | bytes 266272 | tf_op jit(solution)/shard_map/ppermute | solution.py:440
  35.4 1.0 collective-permute-start.4
  36.4 0.0 collective-permute-done.6.refs_6_.refs_4_
  36.4 1.0 collective-permute-start.7
  37.4 43.4 %fold_near.1 = (f32[144,1024]{1,0:T(8,128)S(1)}, f32[144,1024]{1,0:T(8,128)S(1)}, f32[144,1024]{1,0:T(8,128)S(1)}) custom-call(s32[1]{0:T(128)S(6)} %copy.11.start, bf16[1040,128]{1,0:T(8,128)(2,1)S(1)} %collective-permute-done.refs_0_, bf16[1040,128]{1,0:T(8,128)(2,1)S(1)} %collective-permute-done.1.refs_1_, ...), custom_call_target="tpu_custom_call" | custom-call | flops 9663676416 | bytes 1800000 | tf_op jit(solution)/shard_map/fold_near/pallas_call | solution.py:281
  80.8 0.0 collective-permute-done.7.refs_4_.refs_6_
  80.8 15.9 %fold_far.1 = (bf16[144,1024]{1,0:T(8,128)(2,1)}, bf16[144,1024]{1,0:T(8,128)(2,1)}, bf16[144,1024]{1,0:T(8,128)(2,1)}) custom-call(s32[1]{0:T(128)S(6)} %copy.11.start, bf16[1040,128]{1,0:T(8,128)(2,1)S(1)} %collective-permute-done.refs_0_, bf16[1040,128]{1,0:T(8,128)(2,1)S(1)} %collective-permute-done.1.refs_1_, ...), custom_call_target="tpu_custom_call" | custom-call | flops 3221225472 | bytes 600000 | tf_op jit(solution)/shard_map/fold_far/pallas_call | solution.py:281
  96.8 0.0 copy-start.1
  96.8 0.1 collective-permute-start.10
  96.9 2.6 %collective-permute-start.11 = (bf16[144,1024]{1,0:T(8,128)(2,1)}, bf16[144,1024]{1,0:T(8,128)(2,1)S(1)}, u32[]{:S(2)}, u32[]{:S(2)}) collective-permute-start(bf16[144,1024]{1,0:T(8,128)(2,1)} %get-tuple-element.34), channel_id=1, source_target_pairs={{0,32},{8,40},{16,48},{24,56},{32,0},{40,8},{48,16},{56,24},{64,96... | collective-permute-start | bytes 884744 | tf_op jit(solution)/shard_map/ppermute | solution.py:440
  99.5 2.1 %collective-permute-start.12 = (bf16[144,1024]{1,0:T(8,128)(2,1)}, bf16[144,1024]{1,0:T(8,128)(2,1)S(1)}, u32[]{:S(2)}, u32[]{:S(2)}) collective-permute-start(bf16[144,1024]{1,0:T(8,128)(2,1)} %get-tuple-element.33), channel_id=1, source_target_pairs={{0,56},{8,48},{16,40},{24,32},{32,24},{40,16},{48,8},{56,0},{64,12... | collective-permute-start | bytes 884744 | tf_op jit(solution)/shard_map/ppermute | solution.py:440
  101.6 19.3 %fold_own.1.own_ref = f32[144,1024]{1,0:T(8,128)S(1)} custom-call(s32[1]{0:T(128)S(6)} %copy.11.start, bf16[1040,128]{1,0:T(8,128)(2,1)S(1)} %get-tuple-element.25.refs_0_, bf16[2336,128]{1,0:T(8,128)(2,1)S(1)} %get-tuple-element.28.refs_3_.refs_1_, bf16[2336,128]{1,0:T(8,128)(2,1)S(1)} %collective-permute-done.5.refs_4_.refs_2_, ...), custom_call_target="tpu_custom_call" | custom-call | flops 4294967296 | bytes 2400000 | tf_op jit(solution)/shard_map/fold_own/pallas_call | solution.py:281
  120.9 0.0 collective-permute-done.9.near_page
  121.0 1.0 pages.1
  122.0 0.7 reshape.11
  122.7 1.0 merge.1
  (9 shorter events, 0.0 us)
Async XLA Ops:
  2.8 15.9 %collective-permute-start.5 = (bf16[2336,128]{1,0:T(8,128)(2,1)S(1)}, bf16[2336,128]{1,0:T(8,128)(2,1)S(1)}, u32[]{:S(2)}, u32[]{:S(2)}) collective-permute-start(bf16[2336,128]{1,0:T(8,128)(2,1)S(1)} %get-tuple-element.28.refs_3_.refs_1_), channel_id=1, source_target_pairs={{0,8},{8,0},{16,24},{24,16},{32,40},{40,32},{48,56},{56,48},{64,72... | collective-permute-start | bytes 1794056 | tf_op jit(solution)/shard_map/ppermute | solution.py:440
  4.5 20.6 %collective-permute-start.3 = (bf16[1296,128]{1,0:T(8,128)(2,1)S(1)}, bf16[1296,128]{1,0:T(8,128)(2,1)S(1)}, u32[]{:S(2)}, u32[]{:S(2)}) collective-permute-start(bf16[1296,128]{1,0:T(8,128)(2,1)S(1)} %get-tuple-element.26), channel_id=1, source_target_pairs={{0,64},{8,72},{16,80},{24,88},{32,96},{40,104},{48,112},{56,120},{... | collective-permute-start | bytes 995336 | tf_op jit(solution)/shard_map/ppermute | solution.py:440
  7.7 24.7 %collective-permute-start = (bf16[1040,128]{1,0:T(8,128)(2,1)S(1)}, bf16[1040,128]{1,0:T(8,128)(2,1)S(1)}, u32[]{:S(2)}, u32[]{:S(2)}) collective-permute-start(bf16[1040,128]{1,0:T(8,128)(2,1)S(1)} %get-tuple-element.25.refs_0_), channel_id=1, source_target_pairs={{0,56},{8,48},{16,40},{24,32},{32,24},{40,16},{48,8},{56,0},{64,12... | collective-permute-start | bytes 798728 | tf_op jit(solution)/shard_map/ppermute | solution.py:440
  11.3 24.1 %collective-permute-start.1 = (bf16[1040,128]{1,0:T(8,128)(2,1)S(1)}, bf16[1040,128]{1,0:T(8,128)(2,1)S(1)}, u32[]{:S(2)}, u32[]{:S(2)}) collective-permute-start(bf16[1040,128]{1,0:T(8,128)(2,1)S(1)} %get-tuple-element.25.refs_0_), channel_id=1, source_target_pairs={{0,32},{8,40},{16,48},{24,56},{32,0},{40,8},{48,16},{56,24},{64,96... | collective-permute-start | bytes 798728 | tf_op jit(solution)/shard_map/ppermute | solution.py:440
  12.4 0.7 copy-start
  13.0 0.7 copy-start.2
  18.7 17.7 %collective-permute-start.6 = (bf16[1040,128]{1,0:T(8,128)(2,1)S(1)}, bf16[1040,128]{1,0:T(8,128)(2,1)S(1)}, u32[]{:S(2)}, u32[]{:S(2)}) collective-permute-start(bf16[1040,128]{1,0:T(8,128)(2,1)S(1)} %get-tuple-element.29), channel_id=1, source_target_pairs={{0,64},{8,72},{16,80},{24,88},{32,96},{40,104},{48,112},{56,120},{... | collective-permute-start | bytes 798728 | tf_op jit(solution)/shard_map/ppermute | solution.py:440
  21.4 16.0 %collective-permute-start.2 = (bf16[1040,128]{1,0:T(8,128)(2,1)S(1)}, bf16[1040,128]{1,0:T(8,128)(2,1)S(1)}, u32[]{:S(2)}, u32[]{:S(2)}) collective-permute-start(bf16[1040,128]{1,0:T(8,128)(2,1)S(1)} %get-tuple-element.25.refs_0_), channel_id=1, source_target_pairs={{0,24},{8,16},{16,8},{24,0},{32,56},{40,48},{48,40},{56,32},{64,88... | collective-permute-start | bytes 798728 | tf_op jit(solution)/shard_map/ppermute | solution.py:440
  25.1 95.8 %collective-permute-start.8 = (bf16[2,128,128]{2,1,0:T(8,128)(2,1)}, bf16[2,128,128]{2,1,0:T(8,128)(2,1)S(1)}, u32[]{:S(2)}, u32[]{:S(2)}) collective-permute-start(bf16[2,128,128]{2,1,0:T(8,128)(2,1)} %bitcast), channel_id=1, source_target_pairs={{0,128},{16,144},{32,160},{48,176},{64,192},{80,208},{96,224},{112... | collective-permute-start | bytes 196616 | tf_op jit(solution)/shard_map/ppermute | solution.py:457
  32.4 88.5 %collective-permute-start.9 = (bf16[2,128,128]{2,1,0:T(8,128)(2,1)}, bf16[2,128,128]{2,1,0:T(8,128)(2,1)S(1)}, u32[]{:S(2)}, u32[]{:S(2)}) collective-permute-start(bf16[2,128,128]{2,1,0:T(8,128)(2,1)} %bitcast), channel_id=1, source_target_pairs={{8,16},{40,48},{72,80},{104,112},{24,88},{56,120},{88,24},{120,56}... | collective-permute-start | bytes 196616 | tf_op jit(solution)/shard_map/ppermute | solution.py:456
  35.4 45.4 %collective-permute-start.4 = (bf16[1296,128]{1,0:T(8,128)(2,1)S(1)}, bf16[1296,128]{1,0:T(8,128)(2,1)S(1)}, u32[]{:S(2)}, u32[]{:S(2)}) collective-permute-start(bf16[1296,128]{1,0:T(8,128)(2,1)S(1)} %collective-permute-done.3.refs_5_.refs_3_), channel_id=1, source_target_pairs={{0,8},{8,0},{16,24},{24,16},{32,40},{40,32},{48,56},{56,48},{64,72... | collective-permute-start | bytes 995336 | tf_op jit(solution)/shard_map/ppermute | solution.py:440
  36.4 44.4 %collective-permute-start.7 = (bf16[1040,128]{1,0:T(8,128)(2,1)S(1)}, bf16[1040,128]{1,0:T(8,128)(2,1)S(1)}, u32[]{:S(2)}, u32[]{:S(2)}) collective-permute-start(bf16[1040,128]{1,0:T(8,128)(2,1)S(1)} %collective-permute-done.6.refs_6_.refs_4_), channel_id=1, source_target_pairs={{0,8},{8,0},{16,24},{24,16},{32,40},{40,32},{48,56},{56,48},{64,72... | collective-permute-start | bytes 798728 | tf_op jit(solution)/shard_map/ppermute | solution.py:440
  96.8 24.2 %copy-start.1 = (s32[32]{0:T(128)S(1)}, s32[32]{0:T(128)}, u32[]{:S(2)}) copy-start(s32[32]{0:T(128)} %page_rows.3) | copy-start | bytes 388
  96.8 25.9 %collective-permute-start.10 = (bf16[144,1024]{1,0:T(8,128)(2,1)}, bf16[144,1024]{1,0:T(8,128)(2,1)S(1)}, u32[]{:S(2)}, u32[]{:S(2)}) collective-permute-start(bf16[144,1024]{1,0:T(8,128)(2,1)} %get-tuple-element.35), channel_id=1, source_target_pairs={{0,24},{8,16},{16,8},{24,0},{32,56},{40,48},{48,40},{56,32},{64,88... | collective-permute-start | bytes 884744 | tf_op jit(solution)/shard_map/ppermute | solution.py:440
  96.9 25.8 %collective-permute-start.11 = (bf16[144,1024]{1,0:T(8,128)(2,1)}, bf16[144,1024]{1,0:T(8,128)(2,1)S(1)}, u32[]{:S(2)}, u32[]{:S(2)}) collective-permute-start(bf16[144,1024]{1,0:T(8,128)(2,1)} %get-tuple-element.34), channel_id=1, source_target_pairs={{0,32},{8,40},{16,48},{24,56},{32,0},{40,8},{48,16},{56,24},{64,96... | collective-permute-start | bytes 884744 | tf_op jit(solution)/shard_map/ppermute | solution.py:440
  99.5 23.2 %collective-permute-start.12 = (bf16[144,1024]{1,0:T(8,128)(2,1)}, bf16[144,1024]{1,0:T(8,128)(2,1)S(1)}, u32[]{:S(2)}, u32[]{:S(2)}) collective-permute-start(bf16[144,1024]{1,0:T(8,128)(2,1)} %get-tuple-element.33), channel_id=1, source_target_pairs={{0,56},{8,48},{16,40},{24,32},{32,24},{40,16},{48,8},{56,0},{64,12... | collective-permute-start | bytes 884744 | tf_op jit(solution)/shard_map/ppermute | solution.py:440

commit v4 on v3

--- a/solution.py
+++ b/solution.py
@@ -469,7 +469,7 @@
     decode_rows = after(decode_rows, final)
     decode_out = with_pages(page_rows, decode_rows, decoded, far_page, near_page).reshape(decode_query.shape)
     final = after(final, decode_out)
-    prefill_out = merge(final, [from_y, from_z, from_d])
+    prefill_out = merge(final, [from_d, from_z, from_y])
     return (prefill_out, decode_out)
 
 

time: 124 us -> 124 us (level)
  no operation moved by 1% of the time
where the time goes in v4:
time: 124 us
  Pallas kernels  87.9 us (71%)
  starting transfers between devices  29.1 us (23%)
  local copies, waits for them, and re-layouts  2.96 us (2%)
  waiting for transfers between devices  2.36 us (2%)
  between operations  1.44 us (1%)
    pallas_call x3, Pallas kernels, fold(): pl.pallas_call(functools.partial(fold_kernel, n_q=n_q, q_at=q_at, n_in=le...  78.6 us
    ppermute x11, starting transfers between devices, on_device(): send = lambda x, dz, dy: lax.ppermute(x, 'ctx', xor_pairs(dz, dy))  21.1 us
    ppermute x1, starting transfers between devices, on_device(): lax.ppermute(near_source, ('group', 'ctx'), [(n, (n + 16) % 32) for n in...  7.3 us
    pallas_call x1, Pallas kernels, decode(): pl.pallas_call(functools.partial(decode_kernel, row_count=row_count), gri...  5 us
  transfers between devices with their start and end apart: 13, of which 1 were waited for; matrix products, arithmetic and copies ran while one was open for 1% of the time, Pallas kernels for 68%

profile of v4, /device:TPU:2, one launch (start us, length us, event | category | flops | bytes accessed | tf_op | source)
XLA Modules:
  0.0 123.7 jit_solution(6735666162998897663)
XLA Ops:
  0.6 2.2 %prepare.1 = (bf16[1040,128]{1,0:T(8,128)(2,1)S(1)}, bf16[2336,128]{1,0:T(8,128)(2,1)S(1)}, bf16[1296,128]{1,0:T(8,128)(2,1)S(1)}, bf16[1040,128]{1,0:T(8,128)(2,1)S(1)}) custom-call(bf16[1,128,1024]{2,1,0:T(8,128)(2,1)} %query_hbm.1, bf16[1,2,1024,128]{3,2,1,0:T(8,128)(2,1)} %prefix_hbm.1, bf16[1,2,128,128]{3,2,1,0:T(8,128)(2,1)} %stretch_hbm.1), custom_call_target="tpu_custom_call" | custom-call | tf_op jit(solution)/shard_map/prepare/pallas_call | solution.py:82
  2.8 1.7 %collective-permute-start.5 = (bf16[2336,128]{1,0:T(8,128)(2,1)S(1)}, bf16[2336,128]{1,0:T(8,128)(2,1)S(1)}, u32[]{:S(2)}, u32[]{:S(2)}) collective-permute-start(bf16[2336,128]{1,0:T(8,128)(2,1)S(1)} %get-tuple-element.28.refs_3_.refs_1_), channel_id=1, source_target_pairs={{0,8},{8,0},{16,24},{24,16},{32,40},{40,32},{48,56},{56,48},{64,72... | collective-permute-start | bytes 1794056 | tf_op jit(solution)/shard_map/ppermute | solution.py:440
  4.5 3.3 %collective-permute-start.3 = (bf16[1296,128]{1,0:T(8,128)(2,1)S(1)}, bf16[1296,128]{1,0:T(8,128)(2,1)S(1)}, u32[]{:S(2)}, u32[]{:S(2)}) collective-permute-start(bf16[1296,128]{1,0:T(8,128)(2,1)S(1)} %get-tuple-element.26), channel_id=1, source_target_pairs={{0,64},{8,72},{16,80},{24,88},{32,96},{40,104},{48,112},{56,120},{... | collective-permute-start | bytes 995336 | tf_op jit(solution)/shard_map/ppermute | solution.py:440
  7.7 3.5 %collective-permute-start = (bf16[1040,128]{1,0:T(8,128)(2,1)S(1)}, bf16[1040,128]{1,0:T(8,128)(2,1)S(1)}, u32[]{:S(2)}, u32[]{:S(2)}) collective-permute-start(bf16[1040,128]{1,0:T(8,128)(2,1)S(1)} %get-tuple-element.25.refs_0_), channel_id=1, source_target_pairs={{0,56},{8,48},{16,40},{24,32},{32,24},{40,16},{48,8},{56,0},{64,12... | collective-permute-start | bytes 798728 | tf_op jit(solution)/shard_map/ppermute | solution.py:440
  11.3 0.1 collective-permute-start.1
  11.4 1.0 reshape.10.q_ref
  12.4 0.0 copy-start
  12.4 0.6 copy-done
  13.0 0.7 copy-done.2
  13.7 5.0 %decode.1 = (bf16[16,32,128]{2,1,0:T(8,128)(2,1)S(1)}, f32[16,32,128]{2,1,0:T(8,128)S(1)}, f32[16,32,128]{2,1,0:T(8,128)S(1)}) custom-call(s32[32]{0:T(128)S(1)} %copy-done, s32[16]{0:T(128)S(1)} %copy-done.2, bf16[16,32,128]{2,1,0:T(8,128)(2,1)S(1)} %reshape.10.q_ref, bf16[2,16,1024,128]{3,2,1,0:T(8,128)(2,1)} %cache_ref.1, bf16[2,16,4,128]{3,2,1,0:T(4,128)(2,1)} %draft_ref.1), custom_call_target="tpu_custom_call" | custom-call | flops 536870912 | bytes 16777216 | tf_op jit(solution)/shard_map/decode/pallas_call | solution.py:379
  18.7 2.7 %collective-permute-start.6 = (bf16[1040,128]{1,0:T(8,128)(2,1)S(1)}, bf16[1040,128]{1,0:T(8,128)(2,1)S(1)}, u32[]{:S(2)}, u32[]{:S(2)}) collective-permute-start(bf16[1040,128]{1,0:T(8,128)(2,1)S(1)} %get-tuple-element.29), channel_id=1, source_target_pairs={{0,64},{8,72},{16,80},{24,88},{32,96},{40,104},{48,112},{56,120},{... | collective-permute-start | bytes 798728 | tf_op jit(solution)/shard_map/ppermute | solution.py:440
  21.4 3.0 %collective-permute-start.2 = (bf16[1040,128]{1,0:T(8,128)(2,1)S(1)}, bf16[1040,128]{1,0:T(8,128)(2,1)S(1)}, u32[]{:S(2)}, u32[]{:S(2)}) collective-permute-start(bf16[1040,128]{1,0:T(8,128)(2,1)S(1)} %get-tuple-element.25.refs_0_), channel_id=1, source_target_pairs={{0,24},{8,16},{16,8},{24,0},{32,56},{40,48},{48,40},{56,32},{64,88... | collective-permute-start | bytes 798728 | tf_op jit(solution)/shard_map/ppermute | solution.py:440
  25.1 0.0 collective-permute-done.3.refs_5_.refs_3_
  25.1 7.3 %collective-permute-start.8 = (bf16[2,128,128]{2,1,0:T(8,128)(2,1)}, bf16[2,128,128]{2,1,0:T(8,128)(2,1)S(1)}, u32[]{:S(2)}, u32[]{:S(2)}) collective-permute-start(bf16[2,128,128]{2,1,0:T(8,128)(2,1)} %bitcast), channel_id=1, source_target_pairs={{0,128},{16,144},{32,160},{48,176},{64,192},{80,208},{96,224},{112... | collective-permute-start | bytes 196616 | tf_op jit(solution)/shard_map/ppermute | solution.py:457
  32.4 0.0 collective-permute-done.refs_0_
  32.4 0.7 collective-permute-start.9
  33.1 2.3 %collective-permute-done.1.refs_1_ = bf16[1040,128]{1,0:T(8,128)(2,1)S(1)} collective-permute-done((bf16[1040,128]{1,0:T(8,128)(2,1)S(1)}, bf16[1040,128]{1,0:T(8,128)(2,1)S(1)}, u32[]{:S(2)}, u32[]{:S(2)}) %collective-permute-start.1) | collective-permute-done | bytes 266272 | tf_op jit(solution)/shard_map/ppermute | solution.py:440
  35.4 1.0 collective-permute-start.4
  36.4 1.0 collective-permute-start.7
  37.4 0.0 collective-permute-done.2.refs_2_
  37.4 43.4 %fold_near.1 = (f32[144,1024]{1,0:T(8,128)S(1)}, f32[144,1024]{1,0:T(8,128)S(1)}, f32[144,1024]{1,0:T(8,128)S(1)}) custom-call(s32[1]{0:T(128)S(6)} %copy.11.start, bf16[1040,128]{1,0:T(8,128)(2,1)S(1)} %collective-permute-done.refs_0_, bf16[1040,128]{1,0:T(8,128)(2,1)S(1)} %collective-permute-done.1.refs_1_, ...), custom_call_target="tpu_custom_call" | custom-call | flops 9663676416 | bytes 1800000 | tf_op jit(solution)/shard_map/fold_near/pallas_call | solution.py:281
  80.8 0.0 collective-permute-done.7.refs_4_.refs_6_
  80.8 15.9 %fold_far.1 = (bf16[144,1024]{1,0:T(8,128)(2,1)}, bf16[144,1024]{1,0:T(8,128)(2,1)}, bf16[144,1024]{1,0:T(8,128)(2,1)}) custom-call(s32[1]{0:T(128)S(6)} %copy.11.start, bf16[1040,128]{1,0:T(8,128)(2,1)S(1)} %collective-permute-done.refs_0_, bf16[1040,128]{1,0:T(8,128)(2,1)S(1)} %collective-permute-done.1.refs_1_, ...), custom_call_target="tpu_custom_call" | custom-call | flops 3221225472 | bytes 600000 | tf_op jit(solution)/shard_map/fold_far/pallas_call | solution.py:281
  96.8 0.0 copy-start.1
  96.8 2.1 %collective-permute-start.10 = (bf16[144,1024]{1,0:T(8,128)(2,1)}, bf16[144,1024]{1,0:T(8,128)(2,1)S(1)}, u32[]{:S(2)}, u32[]{:S(2)}) collective-permute-start(bf16[144,1024]{1,0:T(8,128)(2,1)} %get-tuple-element.33), channel_id=1, source_target_pairs={{0,56},{8,48},{16,40},{24,32},{32,24},{40,16},{48,8},{56,0},{64,12... | collective-permute-start | bytes 884744 | tf_op jit(solution)/shard_map/ppermute | solution.py:440
  98.9 0.0 collective-permute-start.11
  98.9 2.6 %collective-permute-start.12 = (bf16[144,1024]{1,0:T(8,128)(2,1)}, bf16[144,1024]{1,0:T(8,128)(2,1)S(1)}, u32[]{:S(2)}, u32[]{:S(2)}) collective-permute-start(bf16[144,1024]{1,0:T(8,128)(2,1)} %get-tuple-element.35), channel_id=1, source_target_pairs={{0,24},{8,16},{16,8},{24,0},{32,56},{40,48},{48,40},{56,32},{64,88... | collective-permute-start | bytes 884744 | tf_op jit(solution)/shard_map/ppermute | solution.py:440
  101.6 19.3 %fold_own.1.own_ref = f32[144,1024]{1,0:T(8,128)S(1)} custom-call(s32[1]{0:T(128)S(6)} %copy.11.start, bf16[1040,128]{1,0:T(8,128)(2,1)S(1)} %get-tuple-element.25.refs_0_, bf16[2336,128]{1,0:T(8,128)(2,1)S(1)} %get-tuple-element.28.refs_3_.refs_1_, bf16[2336,128]{1,0:T(8,128)(2,1)S(1)} %collective-permute-done.5.refs_4_.refs_2_, ...), custom_call_target="tpu_custom_call" | custom-call | flops 4294967296 | bytes 2400000 | tf_op jit(solution)/shard_map/fold_own/pallas_call | solution.py:281
  120.9 0.0 collective-permute-done.8.far_page
  121.0 1.0 pages.1
  122.0 0.7 reshape.11
  122.7 1.0 merge.1
  (9 shorter events, 0.0 us)
Async XLA Ops:
  2.8 15.9 %collective-permute-start.5 = (bf16[2336,128]{1,0:T(8,128)(2,1)S(1)}, bf16[2336,128]{1,0:T(8,128)(2,1)S(1)}, u32[]{:S(2)}, u32[]{:S(2)}) collective-permute-start(bf16[2336,128]{1,0:T(8,128)(2,1)S(1)} %get-tuple-element.28.refs_3_.refs_1_), channel_id=1, source_target_pairs={{0,8},{8,0},{16,24},{24,16},{32,40},{40,32},{48,56},{56,48},{64,72... | collective-permute-start | bytes 1794056 | tf_op jit(solution)/shard_map/ppermute | solution.py:440
  4.5 20.6 %collective-permute-start.3 = (bf16[1296,128]{1,0:T(8,128)(2,1)S(1)}, bf16[1296,128]{1,0:T(8,128)(2,1)S(1)}, u32[]{:S(2)}, u32[]{:S(2)}) collective-permute-start(bf16[1296,128]{1,0:T(8,128)(2,1)S(1)} %get-tuple-element.26), channel_id=1, source_target_pairs={{0,64},{8,72},{16,80},{24,88},{32,96},{40,104},{48,112},{56,120},{... | collective-permute-start | bytes 995336 | tf_op jit(solution)/shard_map/ppermute | solution.py:440
  7.7 24.7 %collective-permute-start = (bf16[1040,128]{1,0:T(8,128)(2,1)S(1)}, bf16[1040,128]{1,0:T(8,128)(2,1)S(1)}, u32[]{:S(2)}, u32[]{:S(2)}) collective-permute-start(bf16[1040,128]{1,0:T(8,128)(2,1)S(1)} %get-tuple-element.25.refs_0_), channel_id=1, source_target_pairs={{0,56},{8,48},{16,40},{24,32},{32,24},{40,16},{48,8},{56,0},{64,12... | collective-permute-start | bytes 798728 | tf_op jit(solution)/shard_map/ppermute | solution.py:440
  11.3 24.1 %collective-permute-start.1 = (bf16[1040,128]{1,0:T(8,128)(2,1)S(1)}, bf16[1040,128]{1,0:T(8,128)(2,1)S(1)}, u32[]{:S(2)}, u32[]{:S(2)}) collective-permute-start(bf16[1040,128]{1,0:T(8,128)(2,1)S(1)} %get-tuple-element.25.refs_0_), channel_id=1, source_target_pairs={{0,32},{8,40},{16,48},{24,56},{32,0},{40,8},{48,16},{56,24},{64,96... | collective-permute-start | bytes 798728 | tf_op jit(solution)/shard_map/ppermute | solution.py:440
  12.4 0.7 copy-start
  13.0 0.7 copy-start.2
  18.7 17.7 %collective-permute-start.6 = (bf16[1040,128]{1,0:T(8,128)(2,1)S(1)}, bf16[1040,128]{1,0:T(8,128)(2,1)S(1)}, u32[]{:S(2)}, u32[]{:S(2)}) collective-permute-start(bf16[1040,128]{1,0:T(8,128)(2,1)S(1)} %get-tuple-element.29), channel_id=1, source_target_pairs={{0,64},{8,72},{16,80},{24,88},{32,96},{40,104},{48,112},{56,120},{... | collective-permute-start | bytes 798728 | tf_op jit(solution)/shard_map/ppermute | solution.py:440
  21.4 16.0 %collective-permute-start.2 = (bf16[1040,128]{1,0:T(8,128)(2,1)S(1)}, bf16[1040,128]{1,0:T(8,128)(2,1)S(1)}, u32[]{:S(2)}, u32[]{:S(2)}) collective-permute-start(bf16[1040,128]{1,0:T(8,128)(2,1)S(1)} %get-tuple-element.25.refs_0_), channel_id=1, source_target_pairs={{0,24},{8,16},{16,8},{24,0},{32,56},{40,48},{48,40},{56,32},{64,88... | collective-permute-start | bytes 798728 | tf_op jit(solution)/shard_map/ppermute | solution.py:440
  25.1 95.8 %collective-permute-start.8 = (bf16[2,128,128]{2,1,0:T(8,128)(2,1)}, bf16[2,128,128]{2,1,0:T(8,128)(2,1)S(1)}, u32[]{:S(2)}, u32[]{:S(2)}) collective-permute-start(bf16[2,128,128]{2,1,0:T(8,128)(2,1)} %bitcast), channel_id=1, source_target_pairs={{0,128},{16,144},{32,160},{48,176},{64,192},{80,208},{96,224},{112... | collective-permute-start | bytes 196616 | tf_op jit(solution)/shard_map/ppermute | solution.py:457
  32.4 88.5 %collective-permute-start.9 = (bf16[2,128,128]{2,1,0:T(8,128)(2,1)}, bf16[2,128,128]{2,1,0:T(8,128)(2,1)S(1)}, u32[]{:S(2)}, u32[]{:S(2)}) collective-permute-start(bf16[2,128,128]{2,1,0:T(8,128)(2,1)} %bitcast), channel_id=1, source_target_pairs={{8,16},{40,48},{72,80},{104,112},{24,88},{56,120},{88,24},{120,56}... | collective-permute-start | bytes 196616 | tf_op jit(solution)/shard_map/ppermute | solution.py:456
  35.4 45.4 %collective-permute-start.4 = (bf16[1296,128]{1,0:T(8,128)(2,1)S(1)}, bf16[1296,128]{1,0:T(8,128)(2,1)S(1)}, u32[]{:S(2)}, u32[]{:S(2)}) collective-permute-start(bf16[1296,128]{1,0:T(8,128)(2,1)S(1)} %collective-permute-done.3.refs_5_.refs_3_), channel_id=1, source_target_pairs={{0,8},{8,0},{16,24},{24,16},{32,40},{40,32},{48,56},{56,48},{64,72... | collective-permute-start | bytes 995336 | tf_op jit(solution)/shard_map/ppermute | solution.py:440
  36.4 44.4 %collective-permute-start.7 = (bf16[1040,128]{1,0:T(8,128)(2,1)S(1)}, bf16[1040,128]{1,0:T(8,128)(2,1)S(1)}, u32[]{:S(2)}, u32[]{:S(2)}) collective-permute-start(bf16[1040,128]{1,0:T(8,128)(2,1)S(1)} %collective-permute-done.6.refs_6_.refs_4_), channel_id=1, source_target_pairs={{0,8},{8,0},{16,24},{24,16},{32,40},{40,32},{48,56},{56,48},{64,72... | collective-permute-start | bytes 798728 | tf_op jit(solution)/shard_map/ppermute | solution.py:440
  96.8 24.2 %copy-start.1 = (s32[32]{0:T(128)S(1)}, s32[32]{0:T(128)}, u32[]{:S(2)}) copy-start(s32[32]{0:T(128)} %page_rows.3) | copy-start | bytes 388
  96.8 25.9 %collective-permute-start.10 = (bf16[144,1024]{1,0:T(8,128)(2,1)}, bf16[144,1024]{1,0:T(8,128)(2,1)S(1)}, u32[]{:S(2)}, u32[]{:S(2)}) collective-permute-start(bf16[144,1024]{1,0:T(8,128)(2,1)} %get-tuple-element.33), channel_id=1, source_target_pairs={{0,56},{8,48},{16,40},{24,32},{32,24},{40,16},{48,8},{56,0},{64,12... | collective-permute-start | bytes 884744 | tf_op jit(solution)/shard_map/ppermute | solution.py:440
  98.9 23.8 %collective-permute-start.11 = (bf16[144,1024]{1,0:T(8,128)(2,1)}, bf16[144,1024]{1,0:T(8,128)(2,1)S(1)}, u32[]{:S(2)}, u32[]{:S(2)}) collective-permute-start(bf16[144,1024]{1,0:T(8,128)(2,1)} %get-tuple-element.34), channel_id=1, source_target_pairs={{0,32},{8,40},{16,48},{24,56},{32,0},{40,8},{48,16},{56,24},{64,96... | collective-permute-start | bytes 884744 | tf_op jit(solution)/shard_map/ppermute | solution.py:440
  98.9 23.8 %collective-permute-start.12 = (bf16[144,1024]{1,0:T(8,128)(2,1)}, bf16[144,1024]{1,0:T(8,128)(2,1)S(1)}, u32[]{:S(2)}, u32[]{:S(2)}) collective-permute-start(bf16[144,1024]{1,0:T(8,128)(2,1)} %get-tuple-element.35), channel_id=1, source_target_pairs={{0,24},{8,16},{16,8},{24,0},{32,56},{40,48},{48,40},{56,32},{64,88... | collective-permute-start | bytes 884744 | tf_op jit(solution)/shard_map/ppermute | solution.py:440
